TPU v7x, 128 devices: a whole 4x4x4 slice. The times are simulated.
128 devices in a mesh: seq: 16 (over x, y), head: 8 (over z, core).
Axes of the slice: x: 4, y: 4, z: 4, core: 2. Of those that a mesh axis runs over, the one named last changes fastest.
Arguments:
- queries: bfloat16 [32768, 4096], P('seq', 'head'), may hold values from -24 to 24
- keys: bfloat16 [32768, 4096], P('seq', 'head'), may hold values from -24 to 24
- values: bfloat16 [32768, 4096], P('seq', 'head'), may hold values from -6 to 6
- doc_bounds: int32 [2, 32768], P(None, 'seq'), may hold values from 0 to 32768, as said below
- global_queries: bfloat16 [512, 4096], P(None, 'head'), may hold values from -24 to 24
- global_keys: bfloat16 [512, 4096], P(None, 'head'), may hold values from -24 to 24
- global_span: int32 [2, 512], replicated, may hold values from 0 to 32768, as said below
- global_proj: bfloat16 [4096, 4096], P(None, 'head'), may hold values from -0.09375 to 0.09375
Outputs:
- attended: bfloat16 [32768, 4096], P('seq', 'head')
Inputs may be any that keep to these rules, and one draw needn't show every extreme that they name: `doc_bounds`: documents are runs of consecutive positions of 1 to 4096 tokens, one of exactly 4096, covering the slab; each token's entries bound its own document. `global_span`: each global token's entries are the bounds of one document of doc_bounds that it belongs to.
All inputs are finite; a program needn't handle non-finite values.
Results may differ from a plain program's by a relative error of at most 0.007.
Values may be sent and summed in bfloat16 or wider, within the bound.
A program may use at most 128 MiB of HBM per device.

v0:
```python
import math

import jax
import jax.numpy as jnp
from jax import lax
from jax.sharding import PartitionSpec as P

HD = 128
RADIUS = 512


EXCLUDED = -1e30


def extended(shard, sides, width):
    for axis, dim in sides:
        size, length = (lax.axis_size(axis), shard.shape[dim])
        up = [(i, (i + 1) % size) for i in range(size - 1)]
        down = [(j, i) for i, j in up]
        last = lax.slice_in_dim(shard, length - width, length, axis=dim)
        initial = lax.slice_in_dim(shard, 0, width, axis=dim)
        before = lax.ppermute(last, axis, up)
        after = lax.ppermute(initial, axis, down)
        shard = jnp.concatenate([before, shard, after], axis=dim)
    return shard


def normalize_rows(block):
    widened = block.astype(jnp.float32)
    mean_square = jnp.mean(widened * widened, axis=1, keepdims=True) + 1e-06
    inverse_root = lax.rsqrt(mean_square)
    return (widened * inverse_root).astype(jnp.bfloat16)


def rescale_slab(slab_peak, slab_total, slab_sum, best_peak):
    factor = jnp.exp(slab_peak - best_peak)
    return (slab_total * factor, slab_sum * factor[:, :, None])


def local(queries, keys, values, doc_bounds, global_queries, global_keys, global_span, global_proj):
    tok_rows = queries.shape[0]
    tok_width = queries.shape[1]
    head_dim = HD
    heads_here = tok_width // head_dim
    glob_count = global_queries.shape[0]
    score_scale = 1.0 / math.sqrt(head_dim)
    offset = lax.axis_index("seq") * tok_rows
    positions = offset + jnp.arange(tok_rows, dtype=jnp.int32)
    query_heads = queries.reshape(tok_rows, heads_here, head_dim)
    key_heads = keys.reshape(tok_rows, heads_here, head_dim)
    value_heads = values.reshape(tok_rows, heads_here, head_dim)
    glob_queries = global_queries.reshape(glob_count, heads_here, head_dim)
    scores = (
        jnp.einsum("ghd,thd->ght", glob_queries, key_heads, preferred_element_type=jnp.float32)
        * score_scale
    )
    inside = (positions[None, :] >= global_span[0][:, None]) & (
        positions[None, :] < global_span[1][:, None]
    )
    masked = jnp.where(inside[:, None, :], scores, EXCLUDED)
    slab_peak = jnp.max(masked, axis=2)
    slab_exp = jnp.where(inside[:, None, :], jnp.exp(masked - slab_peak[:, :, None]), 0.0)
    slab_total = jnp.sum(slab_exp, axis=2)
    slab_sum = jnp.einsum(
        "ght,thd->ghd",
        slab_exp.astype(jnp.bfloat16),
        value_heads,
        preferred_element_type=jnp.float32,
    )
    best_peak = lax.pmax(slab_peak, "seq")
    scaled_total, scaled_sum = rescale_slab(slab_peak, slab_total, slab_sum, best_peak)
    summed_rows, summed_total = lax.psum(
        (scaled_sum.reshape(glob_count, tok_width), scaled_total), "seq"
    )
    merged_out = (
        (summed_rows.reshape(glob_count, heads_here, head_dim) / summed_total[:, :, None])
        .reshape(glob_count, tok_width)
        .astype(jnp.bfloat16)
    )
    whole_rows = lax.all_gather(merged_out, "head", axis=1, tiled=True)
    global_values = jnp.dot(
        normalize_rows(whole_rows), global_proj, preferred_element_type=jnp.float32
    ).astype(jnp.bfloat16)
    glob_keys = global_keys.reshape(glob_count, heads_here, head_dim)
    glob_values = global_values.reshape(glob_count, heads_here, head_dim)
    stacked = jnp.stack([keys, values])
    padded = extended(stacked, (("seq", 1),), RADIUS)
    key_padded = padded[0]
    value_padded = padded[1]

    def one_block(block_index):
        block_start = block_index * RADIUS
        query_block = lax.dynamic_slice_in_dim(query_heads, block_start, RADIUS, 0)
        key_block = lax.dynamic_slice_in_dim(key_padded, block_start, 3 * RADIUS, 0).reshape(
            3 * RADIUS, heads_here, head_dim
        )
        value_block = lax.dynamic_slice_in_dim(value_padded, block_start, 3 * RADIUS, 0).reshape(
            3 * RADIUS, heads_here, head_dim
        )
        query_pos = offset + block_start + jnp.arange(RADIUS, dtype=jnp.int32)
        key_pos = offset + block_start - RADIUS + jnp.arange(3 * RADIUS, dtype=jnp.int32)
        doc_start = lax.dynamic_slice_in_dim(doc_bounds[0], block_start, RADIUS, 0)
        doc_end = lax.dynamic_slice_in_dim(doc_bounds[1], block_start, RADIUS, 0)
        admit = (key_pos[None, :] >= doc_start[:, None]) & (key_pos[None, :] < doc_end[:, None])
        admit = admit & (jnp.abs(key_pos[None, :] - query_pos[:, None]) <= RADIUS)
        local_scores = (
            jnp.einsum("qhd,khd->hqk", query_block, key_block, preferred_element_type=jnp.float32)
            * score_scale
        )
        edge_scores = (
            jnp.einsum("qhd,ghd->hqg", query_block, glob_keys, preferred_element_type=jnp.float32)
            * score_scale
        )
        local_masked = jnp.where(admit[None], local_scores, EXCLUDED)
        best_score = jnp.maximum(jnp.max(local_masked, axis=2), jnp.max(edge_scores, axis=2))
        local_exp = jnp.where(admit[None], jnp.exp(local_masked - best_score[:, :, None]), 0.0)
        edge_exp = jnp.exp(edge_scores - best_score[:, :, None])
        total_exp = jnp.sum(local_exp, axis=2) + jnp.sum(edge_exp, axis=2)
        local_weights = (local_exp / total_exp[:, :, None]).astype(jnp.bfloat16)
        edge_weights = (edge_exp / total_exp[:, :, None]).astype(jnp.bfloat16)
        result = jnp.einsum(
            "hqk,khd->qhd", local_weights, value_block, preferred_element_type=jnp.float32
        )
        result = result + jnp.einsum(
            "hqg,ghd->qhd", edge_weights, glob_values, preferred_element_type=jnp.float32
        )
        return result.reshape(RADIUS, tok_width).astype(jnp.bfloat16)

    blocks = lax.map(one_block, jnp.arange(tok_rows // RADIUS, dtype=jnp.int32))
    return blocks.reshape(tok_rows, tok_width)


def solution(mesh):
    in_specs = (
        P("seq", "head"),
        P("seq", "head"),
        P("seq", "head"),
        P(None, "seq"),
        P(None, "head"),
        P(None, "head"),
        P(),
        P(None, "head"),
    )
    out_specs = P("seq", "head")
    return jax.shard_map(local, mesh=mesh, in_specs=in_specs, out_specs=out_specs, check_vma=False)
```

profile of v0, /device:TPU:1, one launch (start us, length us, event | category | flops | bytes accessed | tf_op | source)
XLA Modules:
  0.0 347.1 jit_solution(1143337480296068114)
XLA Ops:
  8.3 9.4 %fusion.20 = (f32[512,4]{0,1:T(4,128)S(1)}, f32[4,2048,512]{2,1,0:T(8,128)}) fusion(pred[512,2048]{0,1:T(8,128)(4,1)S(1)} %compare_and_fusion, bf16[2048,512]{1,0:T(8,128)(2,1)} %param.11, bf16[512,512]{1,0:T(8,128)(2,1)S(1)} %copy-done), kind=kOutput, calls=%fused_computation.36 | convolution fusion | flops 1086322688 | bytes 20455424 | tf_op jit(solution)/shard_map/ghd,thd->ght/dot_general | solution.py:54
  17.7 34.7 %pmax.7 = f32[512,4]{0,1:T(4,128)S(1)} all-reduce(f32[512,4]{0,1:T(4,128)S(1)} %get-tuple-element.179), channel_id=1, replica_groups=mesh['seq'=16,'head'=8] {'seq'}, use_global_device_ids=true, to_apply=%region_1.2 | all-reduce | flops 2048 | bytes 16384 | tf_op jit(solution)/shard_map/pmax | solution.py:70
  52.5 8.2 %fusion.21 = f32[512,4]{0,1:T(4,128)S(1)} fusion(f32[4,2048,512]{2,1,0:T(8,128)} %get-tuple-element.180, f32[512,4]{0,1:T(4,128)S(1)} %get-tuple-element.179, pred[512,2048]{0,1:T(8,128)(4,1)} %copy-done.5), kind=kLoop, calls=%fused_computation.37 | loop fusion | flops 20969472 | bytes 17842176 | tf_op jit(solution)/shard_map/reduce_sum | solution.py:63
  60.7 2.4 copy.31
  63.1 9.7 %fusion.37 = f32[512,4,128]{0,2,1:T(8,128)} fusion(bf16[2048,4,128]{0,2,1:T(8,128)(2,1)} %bitcast.107, f32[4,2048,512]{2,1,0:T(8,128)} %get-tuple-element.180, f32[512,4]{0,1:T(4,128)S(1)} %get-tuple-element.179, pred[512,2048]{0,1:T(8,128)(4,1)} %copy-done.5, f32[512,4]{0,1:T(4,128)S(1)} %get-tuple-element.162), kind=kOutput, calls=%fused_computation.55 | convolution fusion | flops 1094975488 | bytes 20987904 | tf_op jit(solution)/shard_map/ght,thd->ghd/dot_general | solution.py:64
  72.9 29.1 %psum.15 = f32[512,4]{0,1:T(4,128)S(1)} all-reduce(f32[512,4]{0,1:T(4,128)S(1)} %get-tuple-element.161), channel_id=1, replica_groups=mesh['seq'=16,'head'=8] {'seq'}, use_global_device_ids=true, to_apply=%region_4.5 | all-reduce | flops 2048 | bytes 16384 | tf_op jit(solution)/shard_map/psum | solution.py:72
  101.9 61.1 %all-reduce.2.cloned.1.call-done = f32[512,512]{0,1:T(8,128)} async-done(((f32[512,512]{0,1:T(8,128)}), f32[512,512]{0,1:T(8,128)}) %all-reduce.2.cloned.1.call-update) | async-done | bytes 1048592 | tf_op jit(solution)/shard_map/psum | solution.py:72
  163.1 2.2 fusion.43
  165.3 2.7 pad_maximum_fusion.2
  168.0 3.2 collective-permute-start
  172.5 4.0 %copy.17 = bf16[2048,512]{0,1:T(8,128)(2,1)} copy(bf16[2048,512]{1,0:T(8,128)(2,1)} %param.10) | data formatting | bytes 4194304 | tf_op args[0]
  177.0 13.6 %collective-permute-done = bf16[2,512,512]{2,1,0:T(8,128)(2,1)} collective-permute-done((bf16[2,512,512]{2,1,0:T(8,128)(2,1)}, bf16[2,512,512]{2,1,0:T(8,128)(2,1)}, u32[]{:S(2)}, u32[]{:S(2)}) %collective-permute-start) | collective-permute-done | bytes 1048608 | tf_op jit(solution)/shard_map/ppermute | solution.py:22
  190.6 4.8 %collective-permute-done.1 = bf16[2,512,512]{2,1,0:T(8,128)(2,1)} collective-permute-done((bf16[2,512,512]{2,1,0:T(8,128)(2,1)}, bf16[2,512,512]{2,1,0:T(8,128)(2,1)}, u32[]{:S(2)}, u32[]{:S(2)}) %collective-permute-start.1) | collective-permute-done | bytes 1048608 | tf_op jit(solution)/shard_map/ppermute | solution.py:23
  195.4 3.5 %pad_maximum_fusion = bf16[2,3072,512]{2,1,0:T(8,128)(2,1)S(1)} fusion(bf16[2,512,512]{2,1,0:T(8,128)(2,1)} %collective-permute-done.1, bf16[1,2048,512]{2,1,0:T(8,128)(2,1)S(1)} %bitcast.103, bf16[1,2048,512]{2,1,0:T(8,128)(2,1)} %bitcast.106, bf16[2,512,512]{2,1,0:T(8,128)(2,1)} %collective-permute-done), kind=kLoop, calls=%fused_computation.45 | loop fusion | flops 25165824 | bytes 12582912 | tf_op jit(solution)/shard_map/concatenate | solution.py:24
  198.9 3.0 slice_bitcast_fusion
  201.9 3.3 fusion.23
  205.4 5.5 %fusion.40 = bf16[512,512]{0,1:T(8,128)(2,1)} fusion(bf16[4096,512]{1,0:T(8,128)(2,1)} %param.17, bf16[512,4096]{0,1:T(8,128)(2,1)S(1)} %copy-done.6, f32[512]{0:T(512)S(1)} %add_rsqrt_fusion), kind=kOutput, calls=%fused_computation.56 | convolution fusion | flops 2154037248 | bytes 8914944 | tf_op jit(solution)/shard_map/dot_general | solution.py:81
  210.9 128.4 %while.12 = (s32[]{:T(128)}, bf16[4,512,512]{2,1,0:T(8,128)(2,1)}, s32[4]{0:T(128)S(1)}, bf16[3072,512]{1,0:T(8,128)(2,1)}, s32[]{:T(128)}, /*index=5*/s32[2,204...) while((s32[]{:T(128)}, bf16[4,512,512]{2,1,0:T(8,128)(2,1)}, ...), condition=%wide.region_11.12_spmd, body=%wide.region_6.11_spmd.sunk | while | flops 2206988288 | bytes 134935408 | solution.py:129
  212.2 1.7 fusion.76
  213.9 3.7 %constant_dynamic-slice_fusion.7 = (bf16[1536,512]{1,0:T(8,128)(2,1)}, bf16[1536,512]{1,0:T(8,128)(2,1)}) fusion(bf16[3072,512]{1,0:T(8,128)(2,1)} %get-tuple-element.301, s32[]{:T(128)S(6)} %select_n.102, bf16[3072,512]{1,0:T(8,128)(2,1)} %get-tuple-element.297), kind=kLoop, calls=%fused_computation.25.clone.1 | loop fusion | bytes 6291460 | tf_op jit(solution)/shard_map/while/body/eval_jaxpr/dynamic_slice | solution.py:94
  217.6 1.7 copy.54
  219.3 3.8 %fusion.77 = (f32[4,512]{1,0:T(4,128)S(1)}, f32[4,512,1536]{2,1,0:T(8,128)S(1)}) fusion(pred[512,1536]{1,0:T(8,128)(4,1)S(1)} %fusion.76, bf16[1536,4,128]{0,2,1:T(8,128)(2,1)S(1)} %bitcast.99, bf16[2048,4,128]{0,2,1:T(8,128)(2,1)} %get-tuple-element.300, s32[]{:T(128)S(6)} %select_n.101), kind=kOutput, calls=%fused_computation.3.clone.1 | convolution fusion | flops 814741504 | bytes 15474692 | tf_op jit(solution)/shard_map/while/body/eval_jaxpr/qhd,khd->hqk/dot_general | solution.py:107
  223.2 2.1 multiply_reduce_fusion.2
  226.0 4.8 %fusion.78 = f32[4,512]{1,0:T(4,128)S(1)} fusion(f32[4,512,1536]{2,1,0:T(8,128)S(1)} %get-tuple-element.258, f32[4,512]{1,0:T(4,128)S(1)} %max.13, pred[512,1536]{1,0:T(8,128)(4,1)S(1)} %fusion.76), kind=kLoop, calls=%fused_computation.4.clone.1 | loop fusion | flops 15726592 | bytes 13385728 | tf_op jit(solution)/shard_map/while/body/eval_jaxpr/reduce_sum | solution.py:118
  230.9 2.0 fusion.80
  234.5 7.4 %fusion.81 = bf16[512,4,128]{0,2,1:T(8,128)(2,1)S(1)} fusion(f32[512,4,128]{0,2,1:T(8,128)} %fusion.80, bf16[1536,4,128]{0,2,1:T(8,128)(2,1)} %bitcast.100, f32[4,512,1536]{2,1,0:T(8,128)} %copy-done.2, f32[4,512]{1,0:T(4,128)S(1)} %add.133, f32[4,512]{1,0:T(4,128)S(1)} %max.13, pred[512,1536]{1,0:T(8,128)(4,1)S(1)} %fusion.76), kind=kOutput, calls=%fused_computation.16.clone.1 | convolution fusion | flops 824705024 | bytes 16531456 | tf_op jit(solution)/shard_map/while/body/eval_jaxpr/hqk,khd->qhd/dot_general | solution.py:121
  246.0 3.7 %constant_dynamic-slice_fusion.7 = (bf16[1536,512]{1,0:T(8,128)(2,1)}, bf16[1536,512]{1,0:T(8,128)(2,1)}) fusion(bf16[3072,512]{1,0:T(8,128)(2,1)} %get-tuple-element.301, s32[]{:T(128)S(6)} %select_n.102, bf16[3072,512]{1,0:T(8,128)(2,1)} %get-tuple-element.297), kind=kLoop, calls=%fused_computation.25.clone.1 | loop fusion | bytes 6291460 | tf_op jit(solution)/shard_map/while/body/eval_jaxpr/dynamic_slice | solution.py:94
  249.7 1.7 copy.54
  251.4 3.8 %fusion.77 = (f32[4,512]{1,0:T(4,128)S(1)}, f32[4,512,1536]{2,1,0:T(8,128)S(1)}) fusion(pred[512,1536]{1,0:T(8,128)(4,1)S(1)} %fusion.76, bf16[1536,4,128]{0,2,1:T(8,128)(2,1)S(1)} %bitcast.99, bf16[2048,4,128]{0,2,1:T(8,128)(2,1)} %get-tuple-element.300, s32[]{:T(128)S(6)} %select_n.101), kind=kOutput, calls=%fused_computation.3.clone.1 | convolution fusion | flops 814741504 | bytes 15474692 | tf_op jit(solution)/shard_map/while/body/eval_jaxpr/qhd,khd->hqk/dot_general | solution.py:107
  255.3 2.1 multiply_reduce_fusion.2
  258.1 4.8 %fusion.78 = f32[4,512]{1,0:T(4,128)S(1)} fusion(f32[4,512,1536]{2,1,0:T(8,128)S(1)} %get-tuple-element.258, f32[4,512]{1,0:T(4,128)S(1)} %max.13, pred[512,1536]{1,0:T(8,128)(4,1)S(1)} %fusion.76), kind=kLoop, calls=%fused_computation.4.clone.1 | loop fusion | flops 15726592 | bytes 13385728 | tf_op jit(solution)/shard_map/while/body/eval_jaxpr/reduce_sum | solution.py:118
  263.0 2.0 fusion.80
  266.6 7.4 %fusion.81 = bf16[512,4,128]{0,2,1:T(8,128)(2,1)S(1)} fusion(f32[512,4,128]{0,2,1:T(8,128)} %fusion.80, bf16[1536,4,128]{0,2,1:T(8,128)(2,1)} %bitcast.100, f32[4,512,1536]{2,1,0:T(8,128)} %copy-done.2, f32[4,512]{1,0:T(4,128)S(1)} %add.133, f32[4,512]{1,0:T(4,128)S(1)} %max.13, pred[512,1536]{1,0:T(8,128)(4,1)S(1)} %fusion.76), kind=kOutput, calls=%fused_computation.16.clone.1 | convolution fusion | flops 824705024 | bytes 16531456 | tf_op jit(solution)/shard_map/while/body/eval_jaxpr/hqk,khd->qhd/dot_general | solution.py:121
  276.4 1.7 fusion.76
  278.1 3.7 %constant_dynamic-slice_fusion.7 = (bf16[1536,512]{1,0:T(8,128)(2,1)}, bf16[1536,512]{1,0:T(8,128)(2,1)}) fusion(bf16[3072,512]{1,0:T(8,128)(2,1)} %get-tuple-element.301, s32[]{:T(128)S(6)} %select_n.102, bf16[3072,512]{1,0:T(8,128)(2,1)} %get-tuple-element.297), kind=kLoop, calls=%fused_computation.25.clone.1 | loop fusion | bytes 6291460 | tf_op jit(solution)/shard_map/while/body/eval_jaxpr/dynamic_slice | solution.py:94
  281.8 1.7 copy.54
  283.5 3.8 %fusion.77 = (f32[4,512]{1,0:T(4,128)S(1)}, f32[4,512,1536]{2,1,0:T(8,128)S(1)}) fusion(pred[512,1536]{1,0:T(8,128)(4,1)S(1)} %fusion.76, bf16[1536,4,128]{0,2,1:T(8,128)(2,1)S(1)} %bitcast.99, bf16[2048,4,128]{0,2,1:T(8,128)(2,1)} %get-tuple-element.300, s32[]{:T(128)S(6)} %select_n.101), kind=kOutput, calls=%fused_computation.3.clone.1 | convolution fusion | flops 814741504 | bytes 15474692 | tf_op jit(solution)/shard_map/while/body/eval_jaxpr/qhd,khd->hqk/dot_general | solution.py:107
  287.4 2.1 multiply_reduce_fusion.2
  290.2 4.8 %fusion.78 = f32[4,512]{1,0:T(4,128)S(1)} fusion(f32[4,512,1536]{2,1,0:T(8,128)S(1)} %get-tuple-element.258, f32[4,512]{1,0:T(4,128)S(1)} %max.13, pred[512,1536]{1,0:T(8,128)(4,1)S(1)} %fusion.76), kind=kLoop, calls=%fused_computation.4.clone.1 | loop fusion | flops 15726592 | bytes 13385728 | tf_op jit(solution)/shard_map/while/body/eval_jaxpr/reduce_sum | solution.py:118
  295.0 2.0 fusion.80
  298.7 7.4 %fusion.81 = bf16[512,4,128]{0,2,1:T(8,128)(2,1)S(1)} fusion(f32[512,4,128]{0,2,1:T(8,128)} %fusion.80, bf16[1536,4,128]{0,2,1:T(8,128)(2,1)} %bitcast.100, f32[4,512,1536]{2,1,0:T(8,128)} %copy-done.2, f32[4,512]{1,0:T(4,128)S(1)} %add.133, f32[4,512]{1,0:T(4,128)S(1)} %max.13, pred[512,1536]{1,0:T(8,128)(4,1)S(1)} %fusion.76), kind=kOutput, calls=%fused_computation.16.clone.1 | convolution fusion | flops 824705024 | bytes 16531456 | tf_op jit(solution)/shard_map/while/body/eval_jaxpr/hqk,khd->qhd/dot_general | solution.py:121
  310.2 3.7 %constant_dynamic-slice_fusion.7 = (bf16[1536,512]{1,0:T(8,128)(2,1)}, bf16[1536,512]{1,0:T(8,128)(2,1)}) fusion(bf16[3072,512]{1,0:T(8,128)(2,1)} %get-tuple-element.301, s32[]{:T(128)S(6)} %select_n.102, bf16[3072,512]{1,0:T(8,128)(2,1)} %get-tuple-element.297), kind=kLoop, calls=%fused_computation.25.clone.1 | loop fusion | bytes 6291460 | tf_op jit(solution)/shard_map/while/body/eval_jaxpr/dynamic_slice | solution.py:94
  313.9 1.7 copy.54
  315.6 3.8 %fusion.77 = (f32[4,512]{1,0:T(4,128)S(1)}, f32[4,512,1536]{2,1,0:T(8,128)S(1)}) fusion(pred[512,1536]{1,0:T(8,128)(4,1)S(1)} %fusion.76, bf16[1536,4,128]{0,2,1:T(8,128)(2,1)S(1)} %bitcast.99, bf16[2048,4,128]{0,2,1:T(8,128)(2,1)} %get-tuple-element.300, s32[]{:T(128)S(6)} %select_n.101), kind=kOutput, calls=%fused_computation.3.clone.1 | convolution fusion | flops 814741504 | bytes 15474692 | tf_op jit(solution)/shard_map/while/body/eval_jaxpr/qhd,khd->hqk/dot_general | solution.py:107
  319.5 2.1 multiply_reduce_fusion.2
  322.3 4.8 %fusion.78 = f32[4,512]{1,0:T(4,128)S(1)} fusion(f32[4,512,1536]{2,1,0:T(8,128)S(1)} %get-tuple-element.258, f32[4,512]{1,0:T(4,128)S(1)} %max.13, pred[512,1536]{1,0:T(8,128)(4,1)S(1)} %fusion.76), kind=kLoop, calls=%fused_computation.4.clone.1 | loop fusion | flops 15726592 | bytes 13385728 | tf_op jit(solution)/shard_map/while/body/eval_jaxpr/reduce_sum | solution.py:118
  327.1 2.0 fusion.80
  330.8 7.4 %fusion.81 = bf16[512,4,128]{0,2,1:T(8,128)(2,1)S(1)} fusion(f32[512,4,128]{0,2,1:T(8,128)} %fusion.80, bf16[1536,4,128]{0,2,1:T(8,128)(2,1)} %bitcast.100, f32[4,512,1536]{2,1,0:T(8,128)} %copy-done.2, f32[4,512]{1,0:T(4,128)S(1)} %add.133, f32[4,512]{1,0:T(4,128)S(1)} %max.13, pred[512,1536]{1,0:T(8,128)(4,1)S(1)} %fusion.76), kind=kOutput, calls=%fused_computation.16.clone.1 | convolution fusion | flops 824705024 | bytes 16531456 | tf_op jit(solution)/shard_map/while/body/eval_jaxpr/hqk,khd->qhd/dot_general | solution.py:121
  (99 shorter events, 24.3 us)
Async XLA Ops:
  6.5 1.8 copy-start
  6.5 156.5 %all-reduce.2.cloned.1.call-start = ((), (), s32[]{:S(2)}) async-start(), calls=%async_computation | async-start | bytes 2097152 | tf_op jit(solution)/shard_map/psum | solution.py:72
  8.3 9.4 %copy-start.5 = (pred[512,2048]{0,1:T(8,128)(4,1)}, pred[512,2048]{0,1:T(8,128)(4,1)S(1)}, u32[]{:S(2)}) copy-start(pred[512,2048]{0,1:T(8,128)(4,1)S(1)} %compare_and_fusion) | copy-start | bytes 3145732
  52.4 8.2 %copy-start.4 = (bf16[2048,512]{1,0:T(8,128)(2,1)S(1)}, bf16[2048,512]{1,0:T(8,128)(2,1)}, u32[]{:S(2)}) copy-start(bf16[2048,512]{1,0:T(8,128)(2,1)} %param.12) | copy-start | bytes 6291460
  72.8 129.1 %all-gather.2.cloned.1.call-start = ((), (), s32[]{:S(2)}) async-start(), calls=%async_computation.1 | async-start | bytes 4718592 | tf_op jit(solution)/shard_map/all_gather | solution.py:80
  165.3 11.2 %copy-start.7 = (bf16[512,512]{1,0:T(8,128)(2,1)S(1)}, bf16[512,512]{1,0:T(8,128)(2,1)}, u32[]{:S(2)}) copy-start(bf16[512,512]{1,0:T(8,128)(2,1)} %param.15) | copy-start | bytes 1572868
  168.0 22.6 %collective-permute-start = (bf16[2,512,512]{2,1,0:T(8,128)(2,1)}, bf16[2,512,512]{2,1,0:T(8,128)(2,1)}, u32[]{:S(2)}, u32[]{:S(2)}) collective-permute-start(bf16[2,512,512]{2,1,0:T(8,128)(2,1)} %get-tuple-element.175), channel_id=1, source_target_pairs={{0,8},{8,16},{16,24},{24,32},{32,40},{40,48},{48,56},{56,64},{64,7... | collective-permute-start | bytes 3145736 | tf_op jit(solution)/shard_map/ppermute | solution.py:22
  171.2 24.1 %collective-permute-start.1 = (bf16[2,512,512]{2,1,0:T(8,128)(2,1)}, bf16[2,512,512]{2,1,0:T(8,128)(2,1)}, u32[]{:S(2)}, u32[]{:S(2)}) collective-permute-start(bf16[2,512,512]{2,1,0:T(8,128)(2,1)} %get-tuple-element.176), channel_id=1, source_target_pairs={{8,0},{16,8},{24,16},{32,24},{40,32},{48,40},{56,48},{64,56},{72,6... | collective-permute-start | bytes 3145736 | tf_op jit(solution)/shard_map/ppermute | solution.py:23
  201.9 3.4 copy-start.6
  205.4 5.5 %copy-start.8 = (s32[2,2048]{1,0:T(2,128)S(1)}, s32[2,2048]{1,0:T(2,128)}, u32[]{:S(2)}) copy-start(s32[2,2048]{1,0:T(2,128)} %param.13) | copy-start | bytes 49156
  223.2 9.7 %copy-start.2 = (f32[4,512,1536]{2,1,0:T(8,128)}, f32[4,512,1536]{2,1,0:T(8,128)S(1)}, u32[]{:S(2)}) copy-start(f32[4,512,1536]{2,1,0:T(8,128)S(1)} %get-tuple-element.258) | copy-start | bytes 37748740 | tf_op jit(solution)/shard_map/while
  226.0 4.8 %copy-start.9 = (bf16[512,4,128]{0,2,1:T(8,128)(2,1)S(1)}, bf16[512,4,128]{0,2,1:T(8,128)(2,1)}, u32[]{:S(2)}) copy-start(bf16[512,4,128]{0,2,1:T(8,128)(2,1)} %get-tuple-element.303) | copy-start | bytes 1572868 | tf_op jit(solution)/shard_map/while
  230.9 2.1 copy-start.3
  255.3 9.7 %copy-start.2 = (f32[4,512,1536]{2,1,0:T(8,128)}, f32[4,512,1536]{2,1,0:T(8,128)S(1)}, u32[]{:S(2)}) copy-start(f32[4,512,1536]{2,1,0:T(8,128)S(1)} %get-tuple-element.258) | copy-start | bytes 37748740 | tf_op jit(solution)/shard_map/while
  258.1 4.8 %copy-start.9 = (bf16[512,4,128]{0,2,1:T(8,128)(2,1)S(1)}, bf16[512,4,128]{0,2,1:T(8,128)(2,1)}, u32[]{:S(2)}) copy-start(bf16[512,4,128]{0,2,1:T(8,128)(2,1)} %get-tuple-element.303) | copy-start | bytes 1572868 | tf_op jit(solution)/shard_map/while
  262.9 2.1 copy-start.3
  287.4 9.7 %copy-start.2 = (f32[4,512,1536]{2,1,0:T(8,128)}, f32[4,512,1536]{2,1,0:T(8,128)S(1)}, u32[]{:S(2)}) copy-start(f32[4,512,1536]{2,1,0:T(8,128)S(1)} %get-tuple-element.258) | copy-start | bytes 37748740 | tf_op jit(solution)/shard_map/while
  290.2 4.8 %copy-start.9 = (bf16[512,4,128]{0,2,1:T(8,128)(2,1)S(1)}, bf16[512,4,128]{0,2,1:T(8,128)(2,1)}, u32[]{:S(2)}) copy-start(bf16[512,4,128]{0,2,1:T(8,128)(2,1)} %get-tuple-element.303) | copy-start | bytes 1572868 | tf_op jit(solution)/shard_map/while
  295.0 2.1 copy-start.3
  319.5 9.7 %copy-start.2 = (f32[4,512,1536]{2,1,0:T(8,128)}, f32[4,512,1536]{2,1,0:T(8,128)S(1)}, u32[]{:S(2)}) copy-start(f32[4,512,1536]{2,1,0:T(8,128)S(1)} %get-tuple-element.258) | copy-start | bytes 37748740 | tf_op jit(solution)/shard_map/while
  322.3 4.8 %copy-start.9 = (bf16[512,4,128]{0,2,1:T(8,128)(2,1)S(1)}, bf16[512,4,128]{0,2,1:T(8,128)(2,1)}, u32[]{:S(2)}) copy-start(bf16[512,4,128]{0,2,1:T(8,128)(2,1)} %get-tuple-element.303) | copy-start | bytes 1572868 | tf_op jit(solution)/shard_map/while
  327.1 2.1 copy-start.3
  339.3 1.0 copy-start.1
Sparse Core Ops, SparseCore 0:
  72.9 90.1 all-reduce.1
  165.4 33.4 all-gather.1
where the time goes:
time: 351 us; the launch traced here: 347 us
  matrix products  86.2 us (25%)
  waiting for transfers between devices  79.6 us (23%)
  blocking collectives  63.8 us (18%)
  other arithmetic  49.7 us (14%)
  local copies, waits for them, and re-layouts  46.8 us (13%)
  between operations  13.5 us (4%)
  starting transfers between devices  4.54 us (1%)
    psum x1, waiting for transfers between devices, local(): lax.psum((scaled_sum.reshape(glob_count, tok_width), scaled_total), 'seq')  61.1 us
    pmax x1, blocking collectives, local(): best_peak = lax.pmax(slab_peak, 'seq')  34.7 us
    dot_general x4, matrix products, one_block(): jnp.einsum('hqk,khd->qhd', local_weights, value_block, preferred_element_...  29.7 us
    psum x1, blocking collectives, local(): lax.psum((scaled_sum.reshape(glob_count, tok_width), scaled_total), 'seq')  29.1 us
    reduce_sum x8, other arithmetic, one_block(): total_exp = jnp.sum(local_exp, axis=2) + jnp.sum(edge_exp, axis=2)  21.9 us
    dynamic_slice x8, local copies, waits for them, and re-layouts, one_block(): lax.dynamic_slice_in_dim(key_padded, block_start, 3 * RADIUS, 0)  21.8 us
    dot_general x4, matrix products, one_block(): jnp.einsum('qhd,khd->hqk', query_block, key_block, preferred_element_type...  15.3 us
    ppermute x1, waiting for transfers between devices, extended(): before = lax.ppermute(last, axis, up)  13.6 us
  transfers between devices with their start and end apart: 4, of which 3 were waited for; matrix products, arithmetic and copies ran while one was open for 4% of the time, Pallas kernels for 0%

commit v1 on v0

v1 whole, which is shorter than its diff:
```python
import functools
import math

import jax
import jax.numpy as jnp
from jax import lax
from jax.experimental import pallas as pl
from jax.experimental.pallas import tpu as pltpu
from jax.sharding import PartitionSpec as P

HD = 128
RADIUS = 512
HERE = 4
TOK = 2048
GLOB = 512
WIDTH = HERE * HD
TILE = 256
SPAN = TILE + 2 * RADIUS
EXCLUDED = -1e30
LOG2_SCALE = math.log2(math.e) / math.sqrt(HD)
NX = 4
NY = 4
NHEAD = 8
XB = GLOB // NX
YB = XB // NY
MSG = WIDTH + 128
MESH = pl.DeviceIdType.MESH
F32 = jnp.float32
BF16 = jnp.bfloat16


def dot_nt(a, b):
    return lax.dot_general(a, b, (((1,), (1,)), ((), ())), preferred_element_type=F32)


def dot_nn(a, b):
    return jnp.dot(a, b, preferred_element_type=F32)


def twice(k):
    return jnp.concatenate([k, k], axis=1)


def with_ones(v):
    return jnp.concatenate([v, jnp.ones_like(v)], axis=1)


def scaled_parts(q):
    scaled = q.astype(F32) * LOG2_SCALE
    high = scaled.astype(BF16)
    low = (scaled - high.astype(F32)).astype(BF16)
    return jnp.concatenate([high, low], axis=1)


def as_column(row, count):
    return jnp.transpose(jnp.broadcast_to(row.astype(F32), (128, count)))


def combine(parts, rows):
    lane = lax.broadcasted_iota(jnp.int32, (rows, 128), 1)
    stats = [p[:, WIDTH:MSG].astype(F32) for p in parts]
    outs, logs = [], []
    for h in range(HERE):
        mine = (lane >= 3 * h) & (lane < 3 * h + 3)
        lse = [jnp.sum(jnp.where(mine, s, 0.0), axis=1, keepdims=True) for s in stats]
        top = functools.reduce(jnp.maximum, lse)
        weights = [jnp.exp2(x - top) for x in lse]
        total = functools.reduce(jnp.add, weights)
        cols = slice(h * HD, (h + 1) * HD)
        acc = functools.reduce(
            jnp.add, [w * p[:, cols].astype(F32) for w, p in zip(weights, parts)]
        )
        outs.append(acc / total)
        logs.append(top + jnp.log2(total))
    return outs, logs


def put_log(stat, h, log, lane):
    high = log.astype(BF16).astype(F32)
    mid = (log - high).astype(BF16).astype(F32)
    low = log - high - mid
    stat = jnp.where(lane == 3 * h, high, stat)
    stat = jnp.where(lane == 3 * h + 1, mid, stat)
    return jnp.where(lane == 3 * h + 2, low, stat)


def exchange_kernel(
    k_hbm, v_hbm, gq_ref, span_ref, proj_hbm,
    kl_hbm, kr_hbm, vl_hbm, vr_hbm, gv_ref,
    kbuf, vbuf, proj, bias, msg, msg_x, msg2, msg_y, gall,
    load_sems, halo_send, halo_recv, x_send, x_recv, y_send, y_recv,
    z_send, z_recv, gy_send, gy_recv, gx_send, gx_recv,
):
    seq = lax.axis_index("seq")
    head = lax.axis_index("head")
    x, y = seq // NY, seq % NY

    loads = [
        pltpu.make_async_copy(k_hbm, kbuf, load_sems.at[0]),
        pltpu.make_async_copy(v_hbm, vbuf, load_sems.at[1]),
        pltpu.make_async_copy(proj_hbm, proj, load_sems.at[2]),
    ]
    for c in loads:
        c.start()

    right = ((seq + 1) % (NX * NY), head)
    left = ((seq + NX * NY - 1) % (NX * NY), head)
    x_peers = [(((x + d) % NX) * NY + y, head) for d in range(1, NX)]
    y_peers = [(x * NY + (y + d) % NY, head) for d in range(1, NY)]
    z_peers = [(seq, (head + d) % NHEAD) for d in range(1, NHEAD)]
    everyone = [left, right] + x_peers + y_peers + z_peers
    barrier = pltpu.get_barrier_semaphore()
    for peer in everyone:
        pl.semaphore_signal(barrier, inc=1, device_id=peer, device_id_type=MESH)
    pl.semaphore_wait(barrier, len(everyone))

    def remote(src, dst, send, recv, peer):
        return pltpu.make_async_remote_copy(
            src_ref=src, dst_ref=dst, send_sem=send, recv_sem=recv,
            device_id=peer, device_id_type=MESH,
        )

    tail, head_rows = pl.ds(TOK - RADIUS, RADIUS), pl.ds(0, RADIUS)
    halos = [
        remote(k_hbm.at[tail], kl_hbm, halo_send.at[0], halo_recv.at[0], right),
        remote(k_hbm.at[head_rows], kr_hbm, halo_send.at[1], halo_recv.at[1], left),
        remote(v_hbm.at[tail], vl_hbm, halo_send.at[2], halo_recv.at[2], right),
        remote(v_hbm.at[head_rows], vr_hbm, halo_send.at[3], halo_recv.at[3], left),
    ]
    for c in halos:
        c.start()

    offset = (seq * TOK).astype(F32)
    first = as_column(span_ref[0:1, :], GLOB) - offset
    after = as_column(span_ref[1:2, :], GLOB) - offset
    lane_f = lax.broadcasted_iota(jnp.int32, (GLOB, 128), 1).astype(F32)

    @pl.loop(0, TOK // 128)
    def _(j):
        place = lane_f + (j * 128).astype(F32)
        bias[:, pl.ds(pl.multiple_of(j * 128, 128), 128)] = jnp.where(
            (place >= first) & (place < after), 0.0, EXCLUDED
        )

    loads[0].wait()
    loads[1].wait()
    lane = lax.broadcasted_iota(jnp.int32, (GLOB, 128), 1)
    stat = jnp.zeros((GLOB, 128), F32)
    for h in range(HERE):
        cols = slice(h * HD, (h + 1) * HD)
        queries = scaled_parts(gq_ref[:, cols])
        scores = dot_nt(queries, twice(kbuf[:, cols])) + bias[...]
        peak = jnp.max(scores, axis=1, keepdims=True)
        weights = jnp.exp2(scores - peak).astype(BF16)
        acc = dot_nn(weights, with_ones(vbuf[:, cols]))
        msg[:, cols] = (acc[:, :HD] / acc[:, HD:]).astype(BF16)
        stat = put_log(stat, h, peak + jnp.log2(acc[:, HD:]), lane)
    msg[:, WIDTH:MSG] = stat.astype(BF16)

    def x_rows(b):
        return pl.ds(pl.multiple_of(b * XB, XB), XB)

    def y_rows(b):
        return pl.ds(pl.multiple_of(b * YB, YB), YB)

    x_copies = []
    for d in range(1, NX):
        x_copies.append(
            remote(
                msg.at[x_rows((x + d) % NX)], msg_x.at[d - 1],
                x_send.at[d - 1], x_recv.at[d - 1], x_peers[d - 1],
            )
        )
    for c in x_copies:
        c.start()
    for c in x_copies:
        c.wait_recv()
    outs, logs = combine(
        [msg[x_rows(x), :]] + [msg_x[d] for d in range(NX - 1)], XB
    )
    lane = lax.broadcasted_iota(jnp.int32, (XB, 128), 1)
    stat = jnp.zeros((XB, 128), F32)
    for h in range(HERE):
        msg2[:, h * HD:(h + 1) * HD] = outs[h].astype(BF16)
        stat = put_log(stat, h, logs[h], lane)
    msg2[:, WIDTH:MSG] = stat.astype(BF16)

    y_copies = []
    for d in range(1, NY):
        y_copies.append(
            remote(
                msg2.at[y_rows((y + d) % NY)], msg_y.at[d - 1],
                y_send.at[d - 1], y_recv.at[d - 1], y_peers[d - 1],
            )
        )
    for c in y_copies:
        c.start()
    for c in y_copies:
        c.wait_recv()
    outs, _ = combine([msg2[y_rows(y), :]] + [msg_y[d] for d in range(NY - 1)], YB)
    gall[head] = jnp.concatenate([o.astype(BF16) for o in outs], axis=1)

    z_copies = []
    for d in range(1, NHEAD):
        z_copies.append(
            remote(
                gall.at[head], gall.at[head],
                z_send.at[d - 1], z_recv.at[d - 1], z_peers[d - 1],
            )
        )
    for c in z_copies:
        c.start()
    for c in z_copies:
        c.wait_recv()
    squares = jnp.zeros((YB, 1), F32)
    for g in range(NHEAD):
        wide = gall[g].astype(F32)
        squares = squares + jnp.sum(wide * wide, axis=1, keepdims=True)
    inverse = lax.rsqrt(squares / (NHEAD * WIDTH) + 1e-06)
    loads[2].wait()
    total = jnp.zeros((YB, WIDTH), F32)
    for g in range(NHEAD):
        normed = (gall[g].astype(F32) * inverse).astype(BF16)
        total = total + dot_nn(normed, proj[g * WIDTH:(g + 1) * WIDTH, :])
    mine = pl.ds(pl.multiple_of(x * XB + y * YB, YB), YB)
    gv_ref[mine, :] = total.astype(BF16)

    gy_copies = []
    for d in range(1, NY):
        gy_copies.append(
            remote(
                gv_ref.at[mine], gv_ref.at[mine],
                gy_send.at[d - 1], gy_recv.at[d - 1], y_peers[d - 1],
            )
        )
    for c in gy_copies:
        c.start()
    for c in gy_copies:
        c.wait_recv()
    gx_copies = []
    for d in range(1, NX):
        gx_copies.append(
            remote(
                gv_ref.at[x_rows(x)], gv_ref.at[x_rows(x)],
                gx_send.at[d - 1], gx_recv.at[d - 1], x_peers[d - 1],
            )
        )
    for c in gx_copies:
        c.start()
    for c in gx_copies:
        c.wait_recv()
    for c in halos:
        c.wait_recv()
    for c in x_copies + y_copies + z_copies + gy_copies + gx_copies + halos:
        c.wait_send()


def exchange(keys, values, global_queries, global_span, global_proj):
    anyspec = pl.BlockSpec(memory_space=pl.ANY)
    vmem = pl.BlockSpec(memory_space=pltpu.VMEM)
    halo = jax.ShapeDtypeStruct((RADIUS, WIDTH), BF16)
    dma = pltpu.SemaphoreType.DMA
    return pl.pallas_call(
        exchange_kernel,
        out_shape=(halo,) * 4 + (jax.ShapeDtypeStruct((GLOB, WIDTH), BF16),),
        in_specs=[anyspec, anyspec, vmem, vmem, anyspec],
        out_specs=(anyspec,) * 4 + (vmem,),
        scratch_shapes=[
            pltpu.VMEM((TOK, WIDTH), BF16),
            pltpu.VMEM((TOK, WIDTH), BF16),
            pltpu.VMEM((NHEAD * WIDTH, WIDTH), BF16),
            pltpu.VMEM((GLOB, TOK), F32),
            pltpu.VMEM((GLOB, MSG), BF16),
            pltpu.VMEM((NX - 1, XB, MSG), BF16),
            pltpu.VMEM((XB, MSG), BF16),
            pltpu.VMEM((NY - 1, YB, MSG), BF16),
            pltpu.VMEM((NHEAD, YB, WIDTH), BF16),
            dma((3,)), dma((4,)), dma((4,)),
            dma((NX - 1,)), dma((NX - 1,)), dma((NY - 1,)), dma((NY - 1,)),
            dma((NHEAD - 1,)), dma((NHEAD - 1,)),
            dma((NY - 1,)), dma((NY - 1,)), dma((NX - 1,)), dma((NX - 1,)),
        ],
        compiler_params=pltpu.CompilerParams(
            collective_id=0, has_side_effects=True, vmem_limit_bytes=60 * 2**20
        ),
        name="exchange",
    )(keys, values, global_queries, global_span, global_proj)


CHUNKS = (TOK + 2 * RADIUS) // TILE
EARLY = RADIUS // TILE


def attend_kernel(
    q_ref, doc_ref, gk_ref, gv_ref, k_hbm, v_hbm, kl_hbm, kr_hbm, vl_hbm, vr_hbm,
    out_ref, kbuf, vbuf, bias, k_sems, v_sems,
):
    t = pl.program_id(0)
    seq = lax.axis_index("seq")

    def chunk(own, before, behind, buf, sems, c):
        if c < EARLY:
            src = before.at[pl.ds(c * TILE, TILE)]
        elif c < CHUNKS - EARLY:
            src = own.at[pl.ds((c - EARLY) * TILE, TILE)]
        else:
            src = behind.at[pl.ds((c - CHUNKS + EARLY) * TILE, TILE)]
        return pltpu.make_async_copy(src, buf.at[pl.ds(c * TILE, TILE)], sems.at[c])

    k_loads = [chunk(k_hbm, kl_hbm, kr_hbm, kbuf, k_sems, c) for c in range(CHUNKS)]
    v_loads = [chunk(v_hbm, vl_hbm, vr_hbm, vbuf, v_sems, c) for c in range(CHUNKS)]
    span_chunks = SPAN // TILE

    @pl.when(t == 0)
    def _():
        for c in range(CHUNKS):
            k_loads[c].start()
            v_loads[c].start()

    base = (seq * TOK - RADIUS + t * TILE).astype(F32)
    first = as_column(doc_ref[0:1, :], TILE) - base
    after = as_column(doc_ref[1:2, :], TILE) - base
    row = lax.broadcasted_iota(jnp.int32, (TILE, 128), 0).astype(F32)
    lane = lax.broadcasted_iota(jnp.int32, (TILE, 128), 1).astype(F32)
    first = jnp.maximum(first, row)
    after = jnp.minimum(after, row + (2 * RADIUS + 1))
    for j in range(SPAN // 128):
        place = lane + float(j * 128)
        bias[:, j * 128:(j + 1) * 128] = jnp.where(
            (place >= first) & (place < after), 0.0, EXCLUDED
        )

    @pl.when(t == 0)
    def _():
        for c in range(span_chunks):
            k_loads[c].wait()
            v_loads[c].wait()

    for c in range(span_chunks, CHUNKS):
        @pl.when(t == c - span_chunks + 1)
        def _(c=c):
            k_loads[c].wait()
            v_loads[c].wait()

    window = pl.ds(pl.multiple_of(t * TILE, TILE), SPAN)
    for h in range(HERE):
        cols = slice(h * HD, (h + 1) * HD)
        queries = scaled_parts(q_ref[:, cols])
        local = dot_nt(queries, twice(kbuf[window, cols])) + bias[...]
        edge = dot_nt(queries, twice(gk_ref[:, cols]))
        peak = jnp.maximum(
            jnp.max(local, axis=1, keepdims=True), jnp.max(edge, axis=1, keepdims=True)
        )
        local_exp = jnp.exp2(local - peak).astype(BF16)
        edge_exp = jnp.exp2(edge - peak).astype(BF16)
        acc = dot_nn(local_exp, with_ones(vbuf[window, cols]))
        acc = acc + dot_nn(edge_exp, with_ones(gv_ref[:, cols]))
        out_ref[:, cols] = (acc[:, :HD] / acc[:, HD:]).astype(BF16)


def attend(queries, doc_bounds, global_keys, global_values, keys, values, halos):
    anyspec = pl.BlockSpec(memory_space=pl.ANY)
    whole = pl.BlockSpec((GLOB, WIDTH), lambda t: (0, 0))
    tile = pl.BlockSpec((TILE, WIDTH), lambda t: (t, 0))
    dma = pltpu.SemaphoreType.DMA
    return pl.pallas_call(
        attend_kernel,
        out_shape=jax.ShapeDtypeStruct((TOK, WIDTH), BF16),
        grid=(TOK // TILE,),
        in_specs=[tile, pl.BlockSpec((2, TILE), lambda t: (0, t)), whole, whole]
        + [anyspec] * 6,
        out_specs=tile,
        scratch_shapes=[
            pltpu.VMEM((TOK + 2 * RADIUS, WIDTH), BF16),
            pltpu.VMEM((TOK + 2 * RADIUS, WIDTH), BF16),
            pltpu.VMEM((TILE, SPAN), F32),
            dma((CHUNKS,)), dma((CHUNKS,)),
        ],
        compiler_params=pltpu.CompilerParams(vmem_limit_bytes=60 * 2**20),
        name="attend",
    )(queries, doc_bounds, global_keys, global_values, keys, values, *halos)


def local(queries, keys, values, doc_bounds, global_queries, global_keys, global_span, global_proj):
    kl, kr, vl, vr, global_values = exchange(
        keys, values, global_queries, global_span, global_proj
    )
    return attend(
        queries, doc_bounds, global_keys, global_values, keys, values, (kl, kr, vl, vr)
    )


def solution(mesh):
    in_specs = (
        P("seq", "head"),
        P("seq", "head"),
        P("seq", "head"),
        P(None, "seq"),
        P(None, "head"),
        P(None, "head"),
        P(),
        P(None, "head"),
    )
    out_specs = P("seq", "head")
    return jax.shard_map(local, mesh=mesh, in_specs=in_specs, out_specs=out_specs, check_vma=False)
```

time: 351 us -> 95.2 us (0.27)
  Pallas kernels: 0 us -> 93.8 us
  matrix products: 86.2 us -> 0 us
  waiting for transfers between devices: 79.6 us -> 0 us
  blocking collectives: 63.8 us -> 0 us
  other arithmetic: 49.7 us -> 0 us
  local copies, waits for them, and re-layouts: 46.8 us -> 0 us
  between operations: 13.5 us -> 0.01 us
  starting transfers between devices: 4.54 us -> 0 us
    pallas_call x0 -> x2, Pallas kernels: none -> 93.8 us  [the longest x1 62.6 us: exchange(): pl.pallas_call(exchange_kernel, out_shape=(halo,) * 4 + (jax.ShapeDtypeSt...]
    dot_general x19 -> x0, matrix products: 86.2 us -> none  [the longest x4 29.7 us: one_block(): jnp.einsum('hqk,khd->qhd', local_weights, value_block, preferred_element_...]
    psum x1 -> x0, waiting for transfers between devices: 61.1 us -> none  [local(): lax.psum((scaled_sum.reshape(glob_count, tok_width), scaled_total), 'seq')]
    pmax x1 -> x0, blocking collectives: 34.7 us -> none  [local(): best_peak = lax.pmax(slab_peak, 'seq')]
    reduce_sum x10 -> x0, other arithmetic: 33.4 us -> none  [the longest x8 21.9 us: one_block(): total_exp = jnp.sum(local_exp, axis=2) + jnp.sum(edge_exp, axis=2)]
    dynamic_slice x20 -> x0, local copies, waits for them, and re-layouts: 30.7 us -> none  [the longest x8 21.8 us: one_block(): lax.dynamic_slice_in_dim(key_padded, block_start, 3 * RADIUS, 0)]
    psum x1 -> x0, blocking collectives: 29.1 us -> none  [local(): lax.psum((scaled_sum.reshape(glob_count, tok_width), scaled_total), 'seq')]
    ppermute x2 -> x0, waiting for transfers between devices: 18.4 us -> none  [the longest x1 13.6 us: extended(): before = lax.ppermute(last, axis, up)]
  transfers between devices with their start and end apart: 4 -> 0, of which waited for: 3 -> 0; matrix products, arithmetic and copies ran while one was open for 4% -> 0% of each run, Pallas kernels for 0% -> 0%
where the time goes in v1:
time: 95.2 us; the launch traced here: 93.8 us
  Pallas kernels  93.8 us (99%)
    pallas_call x1, Pallas kernels, exchange(): pl.pallas_call(exchange_kernel, out_shape=(halo,) * 4 + (jax.ShapeDtypeSt...  62.6 us
    pallas_call x1, Pallas kernels, attend(): pl.pallas_call(attend_kernel, out_shape=jax.ShapeDtypeStruct((TOK, WIDTH)...  31.2 us

profile of v1, /device:TPU:1, one launch (start us, length us, event | category | flops | bytes accessed | tf_op | source)
XLA Modules:
  0.0 93.8 jit_solution(14643347109688132792)
XLA Ops:
  0.0 62.6 %exchange.1 = (bf16[512,512]{1,0:T(8,128)(2,1)}, bf16[512,512]{1,0:T(8,128)(2,1)}, bf16[512,512]{1,0:T(8,128)(2,1)}, bf16[512,512]{1,0:T(8,128)(2,1)}, bf16[512,512]{1,0:T(8,128)(2,1)}) custom-call(bf16[2048,512]{1,0:T(8,128)(2,1)} %k_hbm.3, bf16[2048,512]{1,0:T(8,128)(2,1)} %v_hbm.3, bf16[512,512]{1,0:T(8,128)(2,1)} %gq_ref.1, s32[2,512]{1,0:T(2,128)} %span_ref.1, ...), custom_call_target="tpu_custom_call" | custom-call | tf_op jit(solution)/shard_map/exchange/pallas_call | solution.py:263
  62.6 31.2 %attend.1 = bf16[2048,512]{1,0:T(8,128)(2,1)} custom-call(bf16[2048,512]{1,0:T(8,128)(2,1)} %q_ref.1, s32[2,2048]{1,0:T(2,128)} %doc_ref.1, bf16[512,512]{1,0:T(8,128)(2,1)} %gk_ref.1, bf16[512,512]{1,0:T(8,128)(2,1)} %get-tuple-element.10.gv_ref, bf16[2048,512]{1,0:T(8,128)(2,1)} %k_hbm.3, bf16[2048,512]{1,0:T(8,128)(2,1)} %v_hbm.3, ...), custom_call_target="tpu_custom_call" | custom-call | tf_op jit(solution)/shard_map/attend/pallas_call | solution.py:366

commit v2 on v0

v2 whole, which is shorter than its diff:
```python
import functools
import math

import jax
import jax.numpy as jnp
from jax import lax
from jax.experimental import pallas as pl
from jax.experimental.pallas import tpu as pltpu
from jax.sharding import PartitionSpec as P

HD = 128
RADIUS = 512
HERE = 4
TOK = 2048
GLOB = 512
WIDTH = HERE * HD
TILE = 256
SPAN = TILE + 2 * RADIUS
EXCLUDED = -1e30
LOG2_SCALE = math.log2(math.e) / math.sqrt(HD)
NX = 4
NY = 4
NHEAD = 8
XB = GLOB // NX
YB = XB // NY
PARTS = HERE + 1
MESH = pl.DeviceIdType.MESH
F32 = jnp.float32
BF16 = jnp.bfloat16


def dot_nt(a, b):
    return lax.dot_general(a, b, (((1,), (1,)), ((), ())), preferred_element_type=F32)


def dot_nn(a, b):
    return jnp.dot(a, b, preferred_element_type=F32)


def twice(k):
    return jnp.concatenate([k, k], axis=1)


def with_ones(v):
    return jnp.concatenate([v, jnp.ones_like(v)], axis=1)


def scaled_parts(q):
    scaled = q.astype(F32) * LOG2_SCALE
    high = scaled.astype(BF16)
    low = (scaled - high.astype(F32)).astype(BF16)
    return jnp.concatenate([high, low], axis=1)


def as_column(row, count):
    return jnp.transpose(jnp.broadcast_to(row.astype(F32), (128, count)))


def combine(parts, rows):
    lane = lax.broadcasted_iota(jnp.int32, (rows, 128), 1)
    stats = [p[HERE].astype(F32) for p in parts]
    outs, logs = [], []
    for h in range(HERE):
        mine = (lane >= 3 * h) & (lane < 3 * h + 3)
        lse = [jnp.sum(jnp.where(mine, s, 0.0), axis=1, keepdims=True) for s in stats]
        top = functools.reduce(jnp.maximum, lse)
        weights = [jnp.exp2(x - top) for x in lse]
        total = functools.reduce(jnp.add, weights)
        acc = functools.reduce(
            jnp.add, [w * p[h].astype(F32) for w, p in zip(weights, parts)]
        )
        outs.append(acc / total)
        logs.append(top + jnp.log2(total))
    return outs, logs


def put_log(stat, h, log, lane):
    high = log.astype(BF16).astype(F32)
    mid = (log - high).astype(BF16).astype(F32)
    low = log - high - mid
    stat = jnp.where(lane == 3 * h, high, stat)
    stat = jnp.where(lane == 3 * h + 1, mid, stat)
    return jnp.where(lane == 3 * h + 2, low, stat)


TILES = TOK // TILE


def kernel(
    gq_ref, gk_ref, span_ref, doc_ref, q_hbm, k_hbm, v_hbm, proj_hbm, out_hbm,
    qbuf, kbuf, vbuf, proj, bias, local_bias, sums, edges, obuf,
    msg, msg_x, msg2, msg_y, gall, gv,
    load_sems, out_sems, halo_send, halo_recv, x_send, x_recv, y_send, y_recv,
    z_send, z_recv, gy_send, gy_recv, gx_send, gx_recv,
):
    seq = lax.axis_index("seq")
    head = lax.axis_index("head")
    x, y = seq // NY, seq % NY
    right = ((seq + 1) % (NX * NY), head)
    left = ((seq + NX * NY - 1) % (NX * NY), head)
    x_peers = [(((x + d) % NX) * NY + y, head) for d in range(1, NX)]
    y_peers = [(x * NY + (y + d) % NY, head) for d in range(1, NY)]
    z_peers = [(seq, (head + d) % NHEAD) for d in range(1, NHEAD)]
    everyone = [left, right] + x_peers + y_peers + z_peers

    def remote(src, dst, send, recv, peer):
        return pltpu.make_async_remote_copy(
            src_ref=src, dst_ref=dst, send_sem=send, recv_sem=recv,
            device_id=peer, device_id_type=MESH,
        )

    def x_rows(b):
        return pl.ds(pl.multiple_of(b * XB, XB), XB)

    def y_rows(b):
        return pl.ds(pl.multiple_of(b * YB, YB), YB)

    own = pl.ds(RADIUS, TOK)
    loads = [
        pltpu.make_async_copy(k_hbm, kbuf.at[own], load_sems.at[0]),
        pltpu.make_async_copy(v_hbm, vbuf.at[own], load_sems.at[1]),
        pltpu.make_async_copy(q_hbm, qbuf, load_sems.at[2]),
        pltpu.make_async_copy(proj_hbm, proj, load_sems.at[3]),
    ]
    front, back = pl.ds(0, RADIUS), pl.ds(TOK - RADIUS, RADIUS)
    before, behind = pl.ds(0, RADIUS), pl.ds(TOK + RADIUS, RADIUS)
    halos = [
        remote(k_hbm.at[back], kbuf.at[before], halo_send.at[0], halo_recv.at[0], right),
        remote(k_hbm.at[front], kbuf.at[behind], halo_send.at[1], halo_recv.at[1], left),
        remote(v_hbm.at[back], vbuf.at[before], halo_send.at[2], halo_recv.at[2], right),
        remote(v_hbm.at[front], vbuf.at[behind], halo_send.at[3], halo_recv.at[3], left),
    ]

    def x_copy(d, h):
        return remote(
            msg.at[h, x_rows((x + d) % NX)], msg_x.at[d - 1, h],
            x_send.at[d - 1, h], x_recv.at[d - 1, h], x_peers[d - 1],
        )

    def y_copy(d):
        return remote(
            msg2.at[:, y_rows((y + d) % NY)], msg_y.at[d - 1],
            y_send.at[d - 1], y_recv.at[d - 1], y_peers[d - 1],
        )

    def z_copy(d):
        return remote(
            gall.at[head], gall.at[head],
            z_send.at[d - 1], z_recv.at[d - 1], z_peers[d - 1],
        )

    mine = pl.ds(pl.multiple_of(x * XB + y * YB, YB), YB)

    def gy_copy(d):
        return remote(
            gv.at[mine], gv.at[mine],
            gy_send.at[d - 1], gy_recv.at[d - 1], y_peers[d - 1],
        )

    def gx_copy(d):
        return remote(
            gv.at[x_rows(x)], gv.at[x_rows(x)],
            gx_send.at[d - 1], gx_recv.at[d - 1], x_peers[d - 1],
        )

    for c in loads:
        c.start()
    barrier = pltpu.get_barrier_semaphore()
    for peer in everyone:
        pl.semaphore_signal(barrier, inc=1, device_id=peer, device_id_type=MESH)
    pl.semaphore_wait(barrier, len(everyone))
    for c in halos:
        c.start()

    offset = (seq * TOK).astype(F32)
    span_first = as_column(span_ref[0:1, :], GLOB) - offset
    span_after = as_column(span_ref[1:2, :], GLOB) - offset
    lane_f = lax.broadcasted_iota(jnp.int32, (GLOB, 128), 1).astype(F32)

    @pl.loop(0, TOK // 128)
    def _(j):
        place = lane_f + (j * 128).astype(F32)
        bias[:, pl.ds(pl.multiple_of(j * 128, 128), 128)] = jnp.where(
            (place >= span_first) & (place < span_after), 0.0, EXCLUDED
        )

    loads[0].wait()
    loads[1].wait()
    lane = lax.broadcasted_iota(jnp.int32, (GLOB, 128), 1)
    stat = jnp.zeros((GLOB, 128), F32)
    for h in range(HERE):
        cols = slice(h * HD, (h + 1) * HD)
        queries = scaled_parts(gq_ref[:, cols])
        scores = dot_nt(queries, twice(kbuf[own, cols])) + bias[...]
        peak = jnp.max(scores, axis=1, keepdims=True)
        weights = jnp.exp2(scores - peak).astype(BF16)
        acc = dot_nn(weights, with_ones(vbuf[own, cols]))
        msg[h] = (acc[:, :HD] / acc[:, HD:]).astype(BF16)
        stat = put_log(stat, h, peak + jnp.log2(acc[:, HD:]), lane)
        for d in (2, 1, 3):
            x_copy(d, h).start()
    msg[HERE] = stat.astype(BF16)
    for d in (2, 1, 3):
        x_copy(d, HERE).start()
    loads[2].wait()

    def after_x():
        for d in range(1, NX):
            for h in range(PARTS):
                x_copy(d, h).wait_recv()
        parts = [[msg[h, x_rows(x), :] for h in range(PARTS)]]
        parts += [[msg_x[d, h] for h in range(PARTS)] for d in range(NX - 1)]
        outs, logs = combine(parts, XB)
        lane = lax.broadcasted_iota(jnp.int32, (XB, 128), 1)
        stat = jnp.zeros((XB, 128), F32)
        for h in range(HERE):
            msg2[h] = outs[h].astype(BF16)
            stat = put_log(stat, h, logs[h], lane)
        msg2[HERE] = stat.astype(BF16)
        for d in range(1, NY):
            y_copy(d).start()

    def after_y():
        for d in range(1, NY):
            y_copy(d).wait_recv()
        parts = [[msg2[h, y_rows(y), :] for h in range(PARTS)]]
        parts += [[msg_y[d, h] for h in range(PARTS)] for d in range(NY - 1)]
        outs, _ = combine(parts, YB)
        gall[head] = jnp.concatenate([o.astype(BF16) for o in outs], axis=1)
        for d in range(1, NHEAD):
            z_copy(d).start()

    def after_z():
        for d in range(1, NHEAD):
            z_copy(d).wait_recv()
        squares = jnp.zeros((YB, 1), F32)
        for g in range(NHEAD):
            wide = gall[g].astype(F32)
            squares = squares + jnp.sum(wide * wide, axis=1, keepdims=True)
        inverse = lax.rsqrt(squares / (NHEAD * WIDTH) + 1e-06)
        loads[3].wait()
        total = jnp.zeros((YB, WIDTH), F32)
        for g in range(NHEAD):
            normed = (gall[g].astype(F32) * inverse).astype(BF16)
            total = total + dot_nn(normed, proj[g * WIDTH:(g + 1) * WIDTH, :])
        gv[mine, :] = total.astype(BF16)
        for d in range(1, NY):
            gy_copy(d).start()

    def after_gy():
        for d in range(1, NY):
            gy_copy(d).wait_recv()
        for d in range(1, NX):
            gx_copy(d).start()

    @pl.loop(0, TILES)
    def _(i):
        half = TILES // 2
        inner = half // 2
        t = jnp.where(i < half, i + inner, jnp.where(i < half + inner, i - half, i))

        @pl.when(i == half)
        def _():
            for c in halos:
                c.wait_recv()

        base = (seq * TOK - RADIUS + t * TILE).astype(F32)
        here = pl.ds(pl.multiple_of(t * TILE, TILE), TILE)
        first = as_column(doc_ref[0:1, here], TILE) - base
        after = as_column(doc_ref[1:2, here], TILE) - base
        row = lax.broadcasted_iota(jnp.int32, (TILE, 128), 0).astype(F32)
        lane = lax.broadcasted_iota(jnp.int32, (TILE, 128), 1).astype(F32)
        first = jnp.maximum(first, row)
        after = jnp.minimum(after, row + (2 * RADIUS + 1))
        for j in range(SPAN // 128):
            place = lane + float(j * 128)
            local_bias[:, j * 128:(j + 1) * 128] = jnp.where(
                (place >= first) & (place < after), 0.0, EXCLUDED
            )
        window = pl.ds(pl.multiple_of(t * TILE, TILE), SPAN)
        for h in range(HERE):
            cols = slice(h * HD, (h + 1) * HD)
            queries = scaled_parts(qbuf[here, cols])
            near = dot_nt(queries, twice(kbuf[window, cols])) + local_bias[...]
            edge = dot_nt(queries, twice(gk_ref[:, cols]))
            peak = jnp.maximum(
                jnp.max(near, axis=1, keepdims=True), jnp.max(edge, axis=1, keepdims=True)
            )
            edges[t, h] = jnp.exp2(edge - peak).astype(BF16)
            near_exp = jnp.exp2(near - peak).astype(BF16)
            sums[t, h] = dot_nn(near_exp, with_ones(vbuf[window, cols]))

        for step, work in enumerate((after_x, after_y, after_z, after_gy)):
            pl.when(i == step)(work)

    for d in range(1, NX):
        gx_copy(d).wait_recv()

    def out_copy(t):
        here = pl.ds(pl.multiple_of(t * TILE, TILE), TILE)
        return pltpu.make_async_copy(obuf.at[here], out_hbm.at[here], out_sems.at[t])

    @pl.loop(0, TILES)
    def _(t):
        here = pl.ds(pl.multiple_of(t * TILE, TILE), TILE)
        for h in range(HERE):
            cols = slice(h * HD, (h + 1) * HD)
            acc = sums[t, h] + dot_nn(edges[t, h], with_ones(gv[:, cols]))
            obuf[here, cols] = (acc[:, :HD] / acc[:, HD:]).astype(BF16)
        out_copy(t).start()

    for t in range(TILES):
        out_copy(t).wait()
    for d in range(1, NX):
        for h in range(PARTS):
            x_copy(d, h).wait_send()
        gx_copy(d).wait_send()
    for d in range(1, NY):
        y_copy(d).wait_send()
        gy_copy(d).wait_send()
    for d in range(1, NHEAD):
        z_copy(d).wait_send()
    for c in halos:
        c.wait_send()


def local(queries, keys, values, doc_bounds, global_queries, global_keys, global_span, global_proj):
    anyspec = pl.BlockSpec(memory_space=pl.ANY)
    vmem = pl.BlockSpec(memory_space=pltpu.VMEM)
    dma = pltpu.SemaphoreType.DMA
    return pl.pallas_call(
        kernel,
        out_shape=jax.ShapeDtypeStruct((TOK, WIDTH), BF16),
        in_specs=[vmem] * 4 + [anyspec] * 4,
        out_specs=anyspec,
        scratch_shapes=[
            pltpu.VMEM((TOK, WIDTH), BF16),
            pltpu.VMEM((TOK + 2 * RADIUS, WIDTH), BF16),
            pltpu.VMEM((TOK + 2 * RADIUS, WIDTH), BF16),
            pltpu.VMEM((NHEAD * WIDTH, WIDTH), BF16),
            pltpu.VMEM((GLOB, TOK), F32),
            pltpu.VMEM((TILE, SPAN), F32),
            pltpu.VMEM((TILES, HERE, TILE, 2 * HD), F32),
            pltpu.VMEM((TILES, HERE, TILE, GLOB), BF16),
            pltpu.VMEM((TOK, WIDTH), BF16),
            pltpu.VMEM((PARTS, GLOB, HD), BF16),
            pltpu.VMEM((NX - 1, PARTS, XB, HD), BF16),
            pltpu.VMEM((PARTS, XB, HD), BF16),
            pltpu.VMEM((NY - 1, PARTS, YB, HD), BF16),
            pltpu.VMEM((NHEAD, YB, WIDTH), BF16),
            pltpu.VMEM((GLOB, WIDTH), BF16),
            dma((4,)), dma((TILES,)), dma((4,)), dma((4,)),
            dma((NX - 1, PARTS)), dma((NX - 1, PARTS)), dma((NY - 1,)), dma((NY - 1,)),
            dma((NHEAD - 1,)), dma((NHEAD - 1,)),
            dma((NY - 1,)), dma((NY - 1,)), dma((NX - 1,)), dma((NX - 1,)),
        ],
        compiler_params=pltpu.CompilerParams(
            collective_id=0, has_side_effects=True, vmem_limit_bytes=63 * 2**20
        ),
        name="attention",
    )(
        global_queries, global_keys, global_span, doc_bounds,
        queries, keys, values, global_proj,
    )


def solution(mesh):
    in_specs = (
        P("seq", "head"),
        P("seq", "head"),
        P("seq", "head"),
        P(None, "seq"),
        P(None, "head"),
        P(None, "head"),
        P(),
        P(None, "head"),
    )
    out_specs = P("seq", "head")
    return jax.shard_map(local, mesh=mesh, in_specs=in_specs, out_specs=out_specs, check_vma=False)
```

time: 351 us -> 75.1 us (0.21); the launches traced: 347 us -> 75 us
  matrix products: 86.2 us -> 0 us
  waiting for transfers between devices: 79.6 us -> 0 us
  Pallas kernels: 0 us -> 71.9 us
  blocking collectives: 63.8 us -> 0 us
  other arithmetic: 49.7 us -> 0 us
  local copies, waits for them, and re-layouts: 46.8 us -> 3.05 us
  between operations: 13.5 us -> 0.01 us
  starting transfers between devices: 4.54 us -> 0 us
    dot_general x19 -> x0, matrix products: 86.2 us -> none  [the longest x4 29.7 us: one_block(): jnp.einsum('hqk,khd->qhd', local_weights, value_block, preferred_element_...]
    pallas_call x0 -> x1, Pallas kernels: none -> 71.9 us  [local(): pl.pallas_call(kernel, out_shape=jax.ShapeDtypeStruct((TOK, WIDTH), BF16)...]
    psum x1 -> x0, waiting for transfers between devices: 61.1 us -> none  [local(): lax.psum((scaled_sum.reshape(glob_count, tok_width), scaled_total), 'seq')]
    pmax x1 -> x0, blocking collectives: 34.7 us -> none  [local(): best_peak = lax.pmax(slab_peak, 'seq')]
    reduce_sum x10 -> x0, other arithmetic: 33.4 us -> none  [the longest x8 21.9 us: one_block(): total_exp = jnp.sum(local_exp, axis=2) + jnp.sum(edge_exp, axis=2)]
    dynamic_slice x20 -> x0, local copies, waits for them, and re-layouts: 30.7 us -> none  [the longest x8 21.8 us: one_block(): lax.dynamic_slice_in_dim(key_padded, block_start, 3 * RADIUS, 0)]
    psum x1 -> x0, blocking collectives: 29.1 us -> none  [local(): lax.psum((scaled_sum.reshape(glob_count, tok_width), scaled_total), 'seq')]
    ppermute x2 -> x0, waiting for transfers between devices: 18.4 us -> none  [the longest x1 13.6 us: extended(): before = lax.ppermute(last, axis, up)]
  transfers between devices with their start and end apart: 4 -> 0, of which waited for: 3 -> 0; matrix products, arithmetic and copies ran while one was open for 4% -> 0% of each run, Pallas kernels for 0% -> 0%
where the time goes in v2:
time: 75.1 us; the launch traced here: 75 us
  Pallas kernels  71.9 us (96%)
  local copies, waits for them, and re-layouts  3.05 us (4%)
    pallas_call x1, Pallas kernels, local(): pl.pallas_call(kernel, out_shape=jax.ShapeDtypeStruct((TOK, WIDTH), BF16)...  71.9 us
    unnamed x1, local copies, waits for them, and re-layouts  3.05 us

profile of v2, /device:TPU:1, one launch (start us, length us, event | category | flops | bytes accessed | tf_op | source)
XLA Modules:
  0.0 75.0 jit_solution(6091853289465114684)
XLA Ops:
  0.0 71.9 %attention.1 = bf16[2048,512]{1,0:T(8,128)(2,1)} custom-call(bf16[512,512]{1,0:T(8,128)(2,1)} %gq_ref.1, bf16[512,512]{1,0:T(8,128)(2,1)} %gk_ref.1, s32[2,512]{1,0:T(2,128)} %span_ref.1, s32[2,2048]{1,0:T(2,128)} %doc_ref.1, bf16[2048,512]{1,0:T(8,128)(2,1)} %q_hbm.1, bf16[2048,512]{1,0:T(8,128)(2,1)} %k_hbm.1, bf16[2048,512]{1,0:T(8,128)(2,1)} %v_hbm.1, ...), custom_call_target="tpu_custom_call" | custom-call | tf_op jit(solution)/shard_map/attention/pallas_call | solution.py:331
  71.9 3.0 %copy.10 = bf16[2048,512]{1,0:T(8,128)(2,1)} copy(bf16[2048,512]{1,0:T(8,128)(2,1)} %attention.1) | data formatting | bytes 4194304

commit v3 on v2

--- a/solution.py
+++ b/solution.py
@@ -88,7 +88,7 @@
 
 def kernel(
     gq_ref, gk_ref, span_ref, doc_ref, q_hbm, k_hbm, v_hbm, proj_hbm, out_hbm,
-    qbuf, kbuf, vbuf, proj, bias, local_bias, sums, edges, obuf,
+    qbuf, kbuf, vbuf, proj, bias, local_bias, sums, edges, factor, obuf,
     msg, msg_x, msg2, msg_y, gall, gv,
     load_sems, out_sems, halo_send, halo_recv, x_send, x_recv, y_send, y_recv,
     z_send, z_recv, gy_send, gy_recv, gx_send, gx_recv,
@@ -169,8 +169,8 @@
     for peer in everyone:
         pl.semaphore_signal(barrier, inc=1, device_id=peer, device_id_type=MESH)
     pl.semaphore_wait(barrier, len(everyone))
-    for c in halos:
-        c.start()
+    halos[0].start()
+    halos[1].start()
 
     offset = (seq * TOK).astype(F32)
     span_first = as_column(span_ref[0:1, :], GLOB) - offset
@@ -197,8 +197,10 @@
         acc = dot_nn(weights, with_ones(vbuf[own, cols]))
         msg[h] = (acc[:, :HD] / acc[:, HD:]).astype(BF16)
         stat = put_log(stat, h, peak + jnp.log2(acc[:, HD:]), lane)
-        for d in (2, 1, 3):
-            x_copy(d, h).start()
+        if h % 2:
+            for d in (2, 1, 3):
+                x_copy(d, h - 1).start()
+                x_copy(d, h).start()
     msg[HERE] = stat.astype(BF16)
     for d in (2, 1, 3):
         x_copy(d, HERE).start()
@@ -229,6 +231,8 @@
         gall[head] = jnp.concatenate([o.astype(BF16) for o in outs], axis=1)
         for d in range(1, NHEAD):
             z_copy(d).start()
+        halos[2].start()
+        halos[3].start()
 
     def after_z():
         for d in range(1, NHEAD):
@@ -253,35 +257,30 @@
         for d in range(1, NX):
             gx_copy(d).start()
 
-    @pl.loop(0, TILES)
-    def _(i):
-        half = TILES // 2
-        inner = half // 2
-        t = jnp.where(i < half, i + inner, jnp.where(i < half + inner, i - half, i))
-
-        @pl.when(i == half)
-        def _():
-            for c in halos:
-                c.wait_recv()
-
-        base = (seq * TOK - RADIUS + t * TILE).astype(F32)
+    def place_bias(t, start, width):
         here = pl.ds(pl.multiple_of(t * TILE, TILE), TILE)
-        first = as_column(doc_ref[0:1, here], TILE) - base
-        after = as_column(doc_ref[1:2, here], TILE) - base
-        row = lax.broadcasted_iota(jnp.int32, (TILE, 128), 0).astype(F32)
+        base = (seq * TOK - RADIUS + start).astype(F32)
+        shift = (t * TILE - start).astype(F32)
+        row = lax.broadcasted_iota(jnp.int32, (TILE, 128), 0).astype(F32) + shift
         lane = lax.broadcasted_iota(jnp.int32, (TILE, 128), 1).astype(F32)
-        first = jnp.maximum(first, row)
-        after = jnp.minimum(after, row + (2 * RADIUS + 1))
-        for j in range(SPAN // 128):
+        first = jnp.maximum(as_column(doc_ref[0:1, here], TILE) - base, row)
+        after = jnp.minimum(
+            as_column(doc_ref[1:2, here], TILE) - base, row + (2 * RADIUS + 1)
+        )
+        for j in range(width // 128):
             place = lane + float(j * 128)
             local_bias[:, j * 128:(j + 1) * 128] = jnp.where(
                 (place >= first) & (place < after), 0.0, EXCLUDED
             )
-        window = pl.ds(pl.multiple_of(t * TILE, TILE), SPAN)
+
+    def own_keys(t, start, width, slot):
+        place_bias(t, start, width)
+        here = pl.ds(pl.multiple_of(t * TILE, TILE), TILE)
+        window = pl.ds(pl.multiple_of(start, TILE), width)
         for h in range(HERE):
             cols = slice(h * HD, (h + 1) * HD)
             queries = scaled_parts(qbuf[here, cols])
-            near = dot_nt(queries, twice(kbuf[window, cols])) + local_bias[...]
+            near = dot_nt(queries, twice(kbuf[window, cols])) + local_bias[:, :width]
             edge = dot_nt(queries, twice(gk_ref[:, cols]))
             peak = jnp.maximum(
                 jnp.max(near, axis=1, keepdims=True), jnp.max(edge, axis=1, keepdims=True)
@@ -289,9 +288,56 @@
             edges[t, h] = jnp.exp2(edge - peak).astype(BF16)
             near_exp = jnp.exp2(near - peak).astype(BF16)
             sums[t, h] = dot_nn(near_exp, with_ones(vbuf[window, cols]))
-
-        for step, work in enumerate((after_x, after_y, after_z, after_gy)):
-            pl.when(i == step)(work)
+            if slot is not None:
+                factor[slot, h] = jnp.broadcast_to(peak, (TILE, HD))
+
+    def halo_keys(t, start, width, slot):
+        place_bias(t, start, width)
+        here = pl.ds(pl.multiple_of(t * TILE, TILE), TILE)
+        window = pl.ds(pl.multiple_of(start, TILE), width)
+        for h in range(HERE):
+            cols = slice(h * HD, (h + 1) * HD)
+            queries = scaled_parts(qbuf[here, cols])
+            near = dot_nt(queries, twice(kbuf[window, cols])) + local_bias[:, :width]
+            peak = jnp.max(near, axis=1, keepdims=True)
+            near_exp = jnp.exp2(near - peak).astype(BF16)
+            more = dot_nn(near_exp, with_ones(vbuf[window, cols]))
+            old = factor[slot, h]
+            top = jnp.maximum(old, peak)
+            down, added = jnp.exp2(old - top), jnp.exp2(peak - top)
+            for c in (slice(0, HD), slice(HD, 2 * HD)):
+                sums[t, h, :, c] = sums[t, h, :, c] * down + more[:, c] * added
+            factor[slot, h] = down
+
+    first_in = RADIUS // TILE
+    last_in = TILES - first_in
+
+    @pl.loop(first_in, last_in)
+    def _(t):
+        own_keys(t, t * TILE, SPAN, None)
+        pl.when(t == first_in)(after_x)
+        pl.when(t == first_in + 2)(after_y)
+
+    far, mid = RADIUS + TILE, RADIUS + 2 * TILE
+
+    @pl.loop(0, 2)
+    def _(i):
+        t = 1 + i * (TILES - 3)
+        own_keys(t, RADIUS + i * (TOK - mid), mid, i)
+        pl.when(i == 0)(after_z)
+        pl.when(i == 1)(after_gy)
+
+    @pl.loop(0, 2)
+    def _(i):
+        own_keys(i * (TILES - 1), RADIUS + i * (TOK - far), far, 2 + i)
+
+    for c in halos:
+        c.wait_recv()
+
+    @pl.loop(0, 2)
+    def _(i):
+        halo_keys(1 + i * (TILES - 3), TILE + i * (TOK + TILE), TILE, i)
+        halo_keys(i * (TILES - 1), i * (TOK + RADIUS), RADIUS, 2 + i)
 
     for d in range(1, NX):
         gx_copy(d).wait_recv()
@@ -300,14 +346,26 @@
         here = pl.ds(pl.multiple_of(t * TILE, TILE), TILE)
         return pltpu.make_async_copy(obuf.at[here], out_hbm.at[here], out_sems.at[t])
 
-    @pl.loop(0, TILES)
-    def _(t):
+    def finish(t, slot):
         here = pl.ds(pl.multiple_of(t * TILE, TILE), TILE)
         for h in range(HERE):
             cols = slice(h * HD, (h + 1) * HD)
-            acc = sums[t, h] + dot_nn(edges[t, h], with_ones(gv[:, cols]))
-            obuf[here, cols] = (acc[:, :HD] / acc[:, HD:]).astype(BF16)
+            edge = dot_nn(edges[t, h], with_ones(gv[:, cols]))
+            upper, lower = edge[:, :HD], edge[:, HD:]
+            if slot is not None:
+                upper, lower = upper * factor[slot, h], lower * factor[slot, h]
+            upper, lower = upper + sums[t, h, :, :HD], lower + sums[t, h, :, HD:]
+            obuf[here, cols] = (upper / lower).astype(BF16)
         out_copy(t).start()
+
+    @pl.loop(first_in, last_in)
+    def _(t):
+        finish(t, None)
+
+    @pl.loop(0, 2)
+    def _(i):
+        finish(1 + i * (TILES - 3), i)
+        finish(i * (TILES - 1), 2 + i)
 
     for t in range(TILES):
         out_copy(t).wait()
@@ -342,6 +400,7 @@
             pltpu.VMEM((TILE, SPAN), F32),
             pltpu.VMEM((TILES, HERE, TILE, 2 * HD), F32),
             pltpu.VMEM((TILES, HERE, TILE, GLOB), BF16),
+            pltpu.VMEM((2 * RADIUS // TILE, HERE, TILE, HD), F32),
             pltpu.VMEM((TOK, WIDTH), BF16),
             pltpu.VMEM((PARTS, GLOB, HD), BF16),
             pltpu.VMEM((NX - 1, PARTS, XB, HD), BF16),

time: 75.1 us -> 68.1 us (0.907)
  Pallas kernels: 71.9 us -> 64.9 us
    pallas_call x1, Pallas kernels: 71.9 us -> 64.9 us  [local(): pl.pallas_call(kernel, out_shape=jax.ShapeDtypeStruct((TOK, WIDTH), BF16)...]
where the time goes in v3:
time: 68.1 us; the launch traced here: 68 us
  Pallas kernels  64.9 us (95%)
  local copies, waits for them, and re-layouts  3.05 us (4%)
    pallas_call x1, Pallas kernels, local(): pl.pallas_call(kernel, out_shape=jax.ShapeDtypeStruct((TOK, WIDTH), BF16)...  64.9 us
    unnamed x1, local copies, waits for them, and re-layouts  3.05 us

profile of v3, /device:TPU:1, one launch (start us, length us, event | category | flops | bytes accessed | tf_op | source)
XLA Modules:
  0.0 68.0 jit_solution(18231452853705632785)
XLA Ops:
  0.0 64.9 %attention.1 = bf16[2048,512]{1,0:T(8,128)(2,1)} custom-call(bf16[512,512]{1,0:T(8,128)(2,1)} %gq_ref.1, bf16[512,512]{1,0:T(8,128)(2,1)} %gk_ref.1, s32[2,512]{1,0:T(2,128)} %span_ref.1, s32[2,2048]{1,0:T(2,128)} %doc_ref.1, bf16[2048,512]{1,0:T(8,128)(2,1)} %q_hbm.1, bf16[2048,512]{1,0:T(8,128)(2,1)} %k_hbm.1, bf16[2048,512]{1,0:T(8,128)(2,1)} %v_hbm.1, ...), custom_call_target="tpu_custom_call" | custom-call | tf_op jit(solution)/shard_map/attention/pallas_call | solution.py:389
  64.9 3.0 %copy.10 = bf16[2048,512]{1,0:T(8,128)(2,1)} copy(bf16[2048,512]{1,0:T(8,128)(2,1)} %attention.1) | data formatting | bytes 4194304

commit v4 on v3

--- a/solution.py
+++ b/solution.py
@@ -24,6 +24,7 @@
 XB = GLOB // NX
 YB = XB // NY
 PARTS = HERE + 1
+SIDE = WIDTH // 2
 MESH = pl.DeviceIdType.MESH
 F32 = jnp.float32
 BF16 = jnp.bfloat16
@@ -88,8 +89,8 @@
 
 def kernel(
     gq_ref, gk_ref, span_ref, doc_ref, q_hbm, k_hbm, v_hbm, proj_hbm, out_hbm,
-    qbuf, kbuf, vbuf, proj, bias, local_bias, sums, edges, factor, obuf,
-    msg, msg_x, msg2, msg_y, gall, gv,
+    qbuf, kbuf, vbuf, proj, bias, local_bias, sums, edges, factor, obuf, scores, weights,
+    msg, msg_x, msg2, msg_y, gall, gv, gk_turned,
     load_sems, out_sems, halo_send, halo_recv, x_send, x_recv, y_send, y_recv,
     z_send, z_recv, gy_send, gy_recv, gx_send, gx_recv,
 ):
@@ -131,10 +132,10 @@
         remote(v_hbm.at[front], vbuf.at[behind], halo_send.at[3], halo_recv.at[3], left),
     ]
 
-    def x_copy(d, h):
+    def x_copy(d):
         return remote(
-            msg.at[h, x_rows((x + d) % NX)], msg_x.at[d - 1, h],
-            x_send.at[d - 1, h], x_recv.at[d - 1, h], x_peers[d - 1],
+            msg.at[:, x_rows((x + d) % NX)], msg_x.at[d - 1],
+            x_send.at[d - 1], x_recv.at[d - 1], x_peers[d - 1],
         )
 
     def y_copy(d):
@@ -149,18 +150,24 @@
             z_send.at[d - 1], z_recv.at[d - 1], z_peers[d - 1],
         )
 
-    mine = pl.ds(pl.multiple_of(x * XB + y * YB, YB), YB)
-
-    def gy_copy(d):
+    mine = [
+        pl.ds(pl.multiple_of(x * XB + y * YB, YB), YB),
+        pl.ds(pl.multiple_of(y * XB + x * YB, YB), YB),
+    ]
+
+    def first_copy(half, d):
         return remote(
-            gv.at[mine], gv.at[mine],
-            gy_send.at[d - 1], gy_recv.at[d - 1], y_peers[d - 1],
-        )
-
-    def gx_copy(d):
+            gv.at[half, mine[half]], gv.at[half, mine[half]],
+            gy_send.at[half, d - 1], gy_recv.at[half, d - 1],
+            (y_peers, x_peers)[half][d - 1],
+        )
+
+    def second_copy(half, d):
+        rows = x_rows((x, y)[half])
         return remote(
-            gv.at[x_rows(x)], gv.at[x_rows(x)],
-            gx_send.at[d - 1], gx_recv.at[d - 1], x_peers[d - 1],
+            gv.at[half, rows], gv.at[half, rows],
+            gx_send.at[half, d - 1], gx_recv.at[half, d - 1],
+            (x_peers, y_peers)[half][d - 1],
         )
 
     for c in loads:
@@ -168,6 +175,11 @@
     barrier = pltpu.get_barrier_semaphore()
     for peer in everyone:
         pl.semaphore_signal(barrier, inc=1, device_id=peer, device_id_type=MESH)
+    for i in range(NX):
+        for j in range(NY):
+            gk_turned[j * XB + i * YB:j * XB + (i + 1) * YB, :] = gk_ref[
+                i * XB + j * YB:i * XB + (j + 1) * YB, SIDE:
+            ]
     pl.semaphore_wait(barrier, len(everyone))
     halos[0].start()
     halos[1].start()
@@ -191,25 +203,27 @@
     for h in range(HERE):
         cols = slice(h * HD, (h + 1) * HD)
         queries = scaled_parts(gq_ref[:, cols])
-        scores = dot_nt(queries, twice(kbuf[own, cols])) + bias[...]
-        peak = jnp.max(scores, axis=1, keepdims=True)
-        weights = jnp.exp2(scores - peak).astype(BF16)
-        acc = dot_nn(weights, with_ones(vbuf[own, cols]))
+        score, weight = scores.at[h % 2], weights.at[h % 2]
+        tops = []
+        for c in range(0, TOK, TILE):
+            part = dot_nt(queries, twice(kbuf[RADIUS + c:RADIUS + c + TILE, cols]))
+            part = part + bias[:, c:c + TILE]
+            score[:, c:c + TILE] = part
+            tops.append(jnp.maximum(part[:, :128], part[:, 128:]))
+        peak = jnp.max(functools.reduce(jnp.maximum, tops), axis=1, keepdims=True)
+        for c in range(0, TOK, TILE):
+            weight[:, c:c + TILE] = jnp.exp2(score[:, c:c + TILE] - peak).astype(BF16)
+        acc = dot_nn(weight[...], with_ones(vbuf[own, cols]))
         msg[h] = (acc[:, :HD] / acc[:, HD:]).astype(BF16)
         stat = put_log(stat, h, peak + jnp.log2(acc[:, HD:]), lane)
-        if h % 2:
-            for d in (2, 1, 3):
-                x_copy(d, h - 1).start()
-                x_copy(d, h).start()
     msg[HERE] = stat.astype(BF16)
     for d in (2, 1, 3):
-        x_copy(d, HERE).start()
+        x_copy(d).start()
     loads[2].wait()
 
     def after_x():
         for d in range(1, NX):
-            for h in range(PARTS):
-                x_copy(d, h).wait_recv()
+            x_copy(d).wait_recv()
         parts = [[msg[h, x_rows(x), :] for h in range(PARTS)]]
         parts += [[msg_x[d, h] for h in range(PARTS)] for d in range(NX - 1)]
         outs, logs = combine(parts, XB)
@@ -247,15 +261,18 @@
         for g in range(NHEAD):
             normed = (gall[g].astype(F32) * inverse).astype(BF16)
             total = total + dot_nn(normed, proj[g * WIDTH:(g + 1) * WIDTH, :])
-        gv[mine, :] = total.astype(BF16)
+        for half in range(2):
+            gv[half, mine[half], :] = total[:, half * SIDE:(half + 1) * SIDE].astype(BF16)
         for d in range(1, NY):
-            gy_copy(d).start()
+            for half in range(2):
+                first_copy(half, d).start()
 
     def after_gy():
-        for d in range(1, NY):
-            gy_copy(d).wait_recv()
-        for d in range(1, NX):
-            gx_copy(d).start()
+        for half in range(2):
+            for d in range(1, NX):
+                first_copy(half, d).wait_recv()
+            for d in range(1, NX):
+                second_copy(half, d).start()
 
     def place_bias(t, start, width):
         here = pl.ds(pl.multiple_of(t * TILE, TILE), TILE)
@@ -280,14 +297,26 @@
         for h in range(HERE):
             cols = slice(h * HD, (h + 1) * HD)
             queries = scaled_parts(qbuf[here, cols])
-            near = dot_nt(queries, twice(kbuf[window, cols])) + local_bias[:, :width]
-            edge = dot_nt(queries, twice(gk_ref[:, cols]))
-            peak = jnp.maximum(
-                jnp.max(near, axis=1, keepdims=True), jnp.max(edge, axis=1, keepdims=True)
-            )
-            edges[t, h] = jnp.exp2(edge - peak).astype(BF16)
-            near_exp = jnp.exp2(near - peak).astype(BF16)
-            sums[t, h] = dot_nn(near_exp, with_ones(vbuf[window, cols]))
+            score, weight = scores.at[h % 2, :TILE], weights.at[h % 2, :TILE]
+            tops = []
+            for c in range(0, width, TILE):
+                rows = pl.ds(pl.multiple_of(start + c, TILE), TILE)
+                part = dot_nt(queries, twice(kbuf[rows, cols])) + local_bias[:, c:c + TILE]
+                score[:, c:c + TILE] = part
+                tops.append(jnp.maximum(part[:, :128], part[:, 128:]))
+            edge_keys = gk_ref[:, cols] if h < 2 else gk_turned[:, (h - 2) * HD:(h - 1) * HD]
+            for c in range(0, GLOB, TILE):
+                part = dot_nt(queries, twice(edge_keys[c:c + TILE]))
+                score[:, width + c:width + c + TILE] = part
+                tops.append(jnp.maximum(part[:, :128], part[:, 128:]))
+            peak = jnp.max(functools.reduce(jnp.maximum, tops), axis=1, keepdims=True)
+            for c in range(0, width, TILE):
+                weight[:, c:c + TILE] = jnp.exp2(score[:, c:c + TILE] - peak).astype(BF16)
+            for c in range(0, GLOB, TILE):
+                edges[t, h, :, c:c + TILE] = jnp.exp2(
+                    score[:, width + c:width + c + TILE] - peak
+                ).astype(BF16)
+            sums[t, h] = dot_nn(weight[:, :width], with_ones(vbuf[window, cols]))
             if slot is not None:
                 factor[slot, h] = jnp.broadcast_to(peak, (TILE, HD))
 
@@ -339,8 +368,9 @@
         halo_keys(1 + i * (TILES - 3), TILE + i * (TOK + TILE), TILE, i)
         halo_keys(i * (TILES - 1), i * (TOK + RADIUS), RADIUS, 2 + i)
 
-    for d in range(1, NX):
-        gx_copy(d).wait_recv()
+    for half in range(2):
+        for d in range(1, NX):
+            second_copy(half, d).wait_recv()
 
     def out_copy(t):
         here = pl.ds(pl.multiple_of(t * TILE, TILE), TILE)
@@ -350,7 +380,7 @@
         here = pl.ds(pl.multiple_of(t * TILE, TILE), TILE)
         for h in range(HERE):
             cols = slice(h * HD, (h + 1) * HD)
-            edge = dot_nn(edges[t, h], with_ones(gv[:, cols]))
+            edge = dot_nn(edges[t, h], with_ones(gv[h // 2, :, (h % 2) * HD:(h % 2 + 1) * HD]))
             upper, lower = edge[:, :HD], edge[:, HD:]
             if slot is not None:
                 upper, lower = upper * factor[slot, h], lower * factor[slot, h]
@@ -370,12 +400,11 @@
     for t in range(TILES):
         out_copy(t).wait()
     for d in range(1, NX):
-        for h in range(PARTS):
-            x_copy(d, h).wait_send()
-        gx_copy(d).wait_send()
-    for d in range(1, NY):
+        x_copy(d).wait_send()
         y_copy(d).wait_send()
-        gy_copy(d).wait_send()
+        for half in range(2):
+            first_copy(half, d).wait_send()
+            second_copy(half, d).wait_send()
     for d in range(1, NHEAD):
         z_copy(d).wait_send()
     for c in halos:
@@ -402,16 +431,19 @@
             pltpu.VMEM((TILES, HERE, TILE, GLOB), BF16),
             pltpu.VMEM((2 * RADIUS // TILE, HERE, TILE, HD), F32),
             pltpu.VMEM((TOK, WIDTH), BF16),
+            pltpu.VMEM((2, GLOB, TOK), F32),
+            pltpu.VMEM((2, GLOB, TOK), BF16),
             pltpu.VMEM((PARTS, GLOB, HD), BF16),
             pltpu.VMEM((NX - 1, PARTS, XB, HD), BF16),
             pltpu.VMEM((PARTS, XB, HD), BF16),
             pltpu.VMEM((NY - 1, PARTS, YB, HD), BF16),
             pltpu.VMEM((NHEAD, YB, WIDTH), BF16),
-            pltpu.VMEM((GLOB, WIDTH), BF16),
+            pltpu.VMEM((2, GLOB, SIDE), BF16),
+            pltpu.VMEM((GLOB, SIDE), BF16),
             dma((4,)), dma((TILES,)), dma((4,)), dma((4,)),
-            dma((NX - 1, PARTS)), dma((NX - 1, PARTS)), dma((NY - 1,)), dma((NY - 1,)),
+            dma((NX - 1,)), dma((NX - 1,)), dma((NY - 1,)), dma((NY - 1,)),
             dma((NHEAD - 1,)), dma((NHEAD - 1,)),
-            dma((NY - 1,)), dma((NY - 1,)), dma((NX - 1,)), dma((NX - 1,)),
+            dma((2, NY - 1)), dma((2, NY - 1)), dma((2, NX - 1)), dma((2, NX - 1)),
         ],
         compiler_params=pltpu.CompilerParams(
             collective_id=0, has_side_effects=True, vmem_limit_bytes=63 * 2**20

time: 68.1 us -> 67.6 us (level)
  no operation moved by 1% of the time
where the time goes in v4:
time: 67.6 us; the launch traced here: 67.4 us
  Pallas kernels  64.4 us (95%)
  local copies, waits for them, and re-layouts  3.05 us (5%)
    pallas_call x1, Pallas kernels, local(): pl.pallas_call(kernel, out_shape=jax.ShapeDtypeStruct((TOK, WIDTH), BF16)...  64.4 us
    unnamed x1, local copies, waits for them, and re-layouts  3.05 us

profile of v4, /device:TPU:1, one launch (start us, length us, event | category | flops | bytes accessed | tf_op | source)
XLA Modules:
  0.0 67.4 jit_solution(2105405873346120287)
XLA Ops:
  0.0 64.4 %attention.1 = bf16[2048,512]{1,0:T(8,128)(2,1)} custom-call(bf16[512,512]{1,0:T(8,128)(2,1)} %gq_ref.1, bf16[512,512]{1,0:T(8,128)(2,1)} %gk_ref.1, s32[2,512]{1,0:T(2,128)} %span_ref.1, s32[2,2048]{1,0:T(2,128)} %doc_ref.1, bf16[2048,512]{1,0:T(8,128)(2,1)} %q_hbm.1, bf16[2048,512]{1,0:T(8,128)(2,1)} %k_hbm.1, bf16[2048,512]{1,0:T(8,128)(2,1)} %v_hbm.1, ...), custom_call_target="tpu_custom_call" | custom-call | tf_op jit(solution)/shard_map/attention/pallas_call | solution.py:418
  64.4 3.0 %copy.10 = bf16[2048,512]{1,0:T(8,128)(2,1)} copy(bf16[2048,512]{1,0:T(8,128)(2,1)} %attention.1) | data formatting | bytes 4194304

commit v5 on v4

--- a/solution.py
+++ b/solution.py
@@ -23,7 +23,11 @@
 NHEAD = 8
 XB = GLOB // NX
 YB = XB // NY
-PARTS = HERE + 1
+PAIR = HERE // 2
+PIECES = 4
+PIECE = RADIUS // PIECES
+HALO_PLAN = (2, 0, 4, 1, 1)
+PARTS = PAIR + 1
 SIDE = WIDTH // 2
 MESH = pl.DeviceIdType.MESH
 F32 = jnp.float32
@@ -59,9 +63,9 @@
 
 def combine(parts, rows):
     lane = lax.broadcasted_iota(jnp.int32, (rows, 128), 1)
-    stats = [p[HERE].astype(F32) for p in parts]
+    stats = [p[PAIR].astype(F32) for p in parts]
     outs, logs = [], []
-    for h in range(HERE):
+    for h in range(PAIR):
         mine = (lane >= 3 * h) & (lane < 3 * h + 3)
         lse = [jnp.sum(jnp.where(mine, s, 0.0), axis=1, keepdims=True) for s in stats]
         top = functools.reduce(jnp.maximum, lse)
@@ -123,25 +127,39 @@
         pltpu.make_async_copy(q_hbm, qbuf, load_sems.at[2]),
         pltpu.make_async_copy(proj_hbm, proj, load_sems.at[3]),
     ]
-    front, back = pl.ds(0, RADIUS), pl.ds(TOK - RADIUS, RADIUS)
-    before, behind = pl.ds(0, RADIUS), pl.ds(TOK + RADIUS, RADIUS)
-    halos = [
-        remote(k_hbm.at[back], kbuf.at[before], halo_send.at[0], halo_recv.at[0], right),
-        remote(k_hbm.at[front], kbuf.at[behind], halo_send.at[1], halo_recv.at[1], left),
-        remote(v_hbm.at[back], vbuf.at[before], halo_send.at[2], halo_recv.at[2], right),
-        remote(v_hbm.at[front], vbuf.at[behind], halo_send.at[3], halo_recv.at[3], left),
-    ]
-
-    def x_copy(d):
+    def halo_pair(c):
+        src, dst = (k_hbm, kbuf) if c < PIECES else (v_hbm, vbuf)
+        at = (c % PIECES) * PIECE
+        return [
+            remote(
+                src.at[pl.ds(TOK - RADIUS + at, PIECE)], dst.at[pl.ds(at, PIECE)],
+                halo_send.at[0, c], halo_recv.at[0, c], right,
+            ),
+            remote(
+                src.at[pl.ds(at, PIECE)], dst.at[pl.ds(TOK + RADIUS + at, PIECE)],
+                halo_send.at[1, c], halo_recv.at[1, c], left,
+            ),
+        ]
+
+    def send_halos(stage):
+        first = sum(HALO_PLAN[:stage])
+        for c in range(first, first + HALO_PLAN[stage]):
+            for copy in halo_pair(c):
+                copy.start()
+
+    block = (x, y)
+    line_peers = (x_peers, y_peers)
+
+    def part_copy(half, d):
         return remote(
-            msg.at[:, x_rows((x + d) % NX)], msg_x.at[d - 1],
-            x_send.at[d - 1], x_recv.at[d - 1], x_peers[d - 1],
-        )
-
-    def y_copy(d):
+            msg.at[half, :, x_rows((block[half] + d) % NX)], msg_x.at[half, d - 1],
+            x_send.at[half, d - 1], x_recv.at[half, d - 1], line_peers[half][d - 1],
+        )
+
+    def merge_copy(half, d):
         return remote(
-            msg2.at[:, y_rows((y + d) % NY)], msg_y.at[d - 1],
-            y_send.at[d - 1], y_recv.at[d - 1], y_peers[d - 1],
+            msg2.at[half, :, y_rows((block[1 - half] + d) % NY)], msg_y.at[half, d - 1],
+            y_send.at[half, d - 1], y_recv.at[half, d - 1], line_peers[1 - half][d - 1],
         )
 
     def z_copy(d):
@@ -181,8 +199,7 @@
                 i * XB + j * YB:i * XB + (j + 1) * YB, SIDE:
             ]
     pl.semaphore_wait(barrier, len(everyone))
-    halos[0].start()
-    halos[1].start()
+    send_halos(0)
 
     offset = (seq * TOK).astype(F32)
     span_first = as_column(span_ref[0:1, :], GLOB) - offset
@@ -199,8 +216,20 @@
     loads[0].wait()
     loads[1].wait()
     lane = lax.broadcasted_iota(jnp.int32, (GLOB, 128), 1)
-    stat = jnp.zeros((GLOB, 128), F32)
+    stats = [jnp.zeros((GLOB, 128), F32)] * 2
+
+    def put_rows(half, part, rows):
+        if half == 0:
+            msg[half, part] = rows
+            return
+        for i in range(NX):
+            for j in range(NY):
+                msg[half, part, j * XB + i * YB:j * XB + (i + 1) * YB, :] = rows[
+                    i * XB + j * YB:i * XB + (j + 1) * YB
+                ]
+
     for h in range(HERE):
+        half, part_at = h // PAIR, h % PAIR
         cols = slice(h * HD, (h + 1) * HD)
         queries = scaled_parts(gq_ref[:, cols])
         score, weight = scores.at[h % 2], weights.at[h % 2]
@@ -214,39 +243,49 @@
         for c in range(0, TOK, TILE):
             weight[:, c:c + TILE] = jnp.exp2(score[:, c:c + TILE] - peak).astype(BF16)
         acc = dot_nn(weight[...], with_ones(vbuf[own, cols]))
-        msg[h] = (acc[:, :HD] / acc[:, HD:]).astype(BF16)
-        stat = put_log(stat, h, peak + jnp.log2(acc[:, HD:]), lane)
-    msg[HERE] = stat.astype(BF16)
+        put_rows(half, part_at, (acc[:, :HD] / acc[:, HD:]).astype(BF16))
+        stats[half] = put_log(stats[half], part_at, peak + jnp.log2(acc[:, HD:]), lane)
+    for half in range(2):
+        put_rows(half, PAIR, stats[half].astype(BF16))
     for d in (2, 1, 3):
-        x_copy(d).start()
+        for half in range(2):
+            part_copy(half, d).start()
     loads[2].wait()
 
     def after_x():
-        for d in range(1, NX):
-            x_copy(d).wait_recv()
-        parts = [[msg[h, x_rows(x), :] for h in range(PARTS)]]
-        parts += [[msg_x[d, h] for h in range(PARTS)] for d in range(NX - 1)]
-        outs, logs = combine(parts, XB)
         lane = lax.broadcasted_iota(jnp.int32, (XB, 128), 1)
-        stat = jnp.zeros((XB, 128), F32)
-        for h in range(HERE):
-            msg2[h] = outs[h].astype(BF16)
-            stat = put_log(stat, h, logs[h], lane)
-        msg2[HERE] = stat.astype(BF16)
+        for half in range(2):
+            for d in range(1, NX):
+                part_copy(half, d).wait_recv()
+        for half in range(2):
+            mine = x_rows(block[half])
+            parts = [[msg[half, h, mine, :] for h in range(PARTS)]]
+            parts += [[msg_x[half, d, h] for h in range(PARTS)] for d in range(NX - 1)]
+            outs, logs = combine(parts, XB)
+            stat = jnp.zeros((XB, 128), F32)
+            for h in range(PAIR):
+                msg2[half, h] = outs[h].astype(BF16)
+                stat = put_log(stat, h, logs[h], lane)
+            msg2[half, PAIR] = stat.astype(BF16)
         for d in range(1, NY):
-            y_copy(d).start()
+            for half in range(2):
+                merge_copy(half, d).start()
+        send_halos(1)
 
     def after_y():
-        for d in range(1, NY):
-            y_copy(d).wait_recv()
-        parts = [[msg2[h, y_rows(y), :] for h in range(PARTS)]]
-        parts += [[msg_y[d, h] for h in range(PARTS)] for d in range(NY - 1)]
-        outs, _ = combine(parts, YB)
-        gall[head] = jnp.concatenate([o.astype(BF16) for o in outs], axis=1)
+        for half in range(2):
+            for d in range(1, NY):
+                merge_copy(half, d).wait_recv()
+        merged = []
+        for half in range(2):
+            mine = y_rows(block[1 - half])
+            parts = [[msg2[half, h, mine, :] for h in range(PARTS)]]
+            parts += [[msg_y[half, d, h] for h in range(PARTS)] for d in range(NY - 1)]
+            merged += combine(parts, YB)[0]
+        gall[head] = jnp.concatenate([o.astype(BF16) for o in merged], axis=1)
         for d in range(1, NHEAD):
             z_copy(d).start()
-        halos[2].start()
-        halos[3].start()
+        send_halos(2)
 
     def after_z():
         for d in range(1, NHEAD):
@@ -266,6 +305,7 @@
         for d in range(1, NY):
             for half in range(2):
                 first_copy(half, d).start()
+        send_halos(3)
 
     def after_gy():
         for half in range(2):
@@ -273,6 +313,7 @@
                 first_copy(half, d).wait_recv()
             for d in range(1, NX):
                 second_copy(half, d).start()
+        send_halos(4)
 
     def place_bias(t, start, width):
         here = pl.ds(pl.multiple_of(t * TILE, TILE), TILE)
@@ -344,7 +385,7 @@
     @pl.loop(first_in, last_in)
     def _(t):
         own_keys(t, t * TILE, SPAN, None)
-        pl.when(t == first_in)(after_x)
+        pl.when(t == first_in + 1)(after_x)
         pl.when(t == first_in + 2)(after_y)
 
     far, mid = RADIUS + TILE, RADIUS + 2 * TILE
@@ -360,8 +401,9 @@
     def _(i):
         own_keys(i * (TILES - 1), RADIUS + i * (TOK - far), far, 2 + i)
 
-    for c in halos:
-        c.wait_recv()
+    for c in range(2 * PIECES):
+        for copy in halo_pair(c):
+            copy.wait_recv()
 
     @pl.loop(0, 2)
     def _(i):
@@ -400,15 +442,16 @@
     for t in range(TILES):
         out_copy(t).wait()
     for d in range(1, NX):
-        x_copy(d).wait_send()
-        y_copy(d).wait_send()
-        for half in range(2):
+        for half in range(2):
+            part_copy(half, d).wait_send()
+            merge_copy(half, d).wait_send()
             first_copy(half, d).wait_send()
             second_copy(half, d).wait_send()
     for d in range(1, NHEAD):
         z_copy(d).wait_send()
-    for c in halos:
-        c.wait_send()
+    for c in range(2 * PIECES):
+        for copy in halo_pair(c):
+            copy.wait_send()
 
 
 def local(queries, keys, values, doc_bounds, global_queries, global_keys, global_span, global_proj):
@@ -433,15 +476,15 @@
             pltpu.VMEM((TOK, WIDTH), BF16),
             pltpu.VMEM((2, GLOB, TOK), F32),
             pltpu.VMEM((2, GLOB, TOK), BF16),
-            pltpu.VMEM((PARTS, GLOB, HD), BF16),
-            pltpu.VMEM((NX - 1, PARTS, XB, HD), BF16),
-            pltpu.VMEM((PARTS, XB, HD), BF16),
-            pltpu.VMEM((NY - 1, PARTS, YB, HD), BF16),
+            pltpu.VMEM((2, PARTS, GLOB, HD), BF16),
+            pltpu.VMEM((2, NX - 1, PARTS, XB, HD), BF16),
+            pltpu.VMEM((2, PARTS, XB, HD), BF16),
+            pltpu.VMEM((2, NY - 1, PARTS, YB, HD), BF16),
             pltpu.VMEM((NHEAD, YB, WIDTH), BF16),
             pltpu.VMEM((2, GLOB, SIDE), BF16),
             pltpu.VMEM((GLOB, SIDE), BF16),
-            dma((4,)), dma((TILES,)), dma((4,)), dma((4,)),
-            dma((NX - 1,)), dma((NX - 1,)), dma((NY - 1,)), dma((NY - 1,)),
+            dma((4,)), dma((TILES,)), dma((2, 2 * PIECES)), dma((2, 2 * PIECES)),
+            dma((2, NX - 1)), dma((2, NX - 1)), dma((2, NY - 1)), dma((2, NY - 1)),
             dma((NHEAD - 1,)), dma((NHEAD - 1,)),
             dma((2, NY - 1)), dma((2, NY - 1)), dma((2, NX - 1)), dma((2, NX - 1)),
         ],

time: 67.6 us -> 65.4 us (0.967)
  Pallas kernels: 64.4 us -> 62.2 us
    pallas_call x1, Pallas kernels: 64.4 us -> 62.2 us  [local(): pl.pallas_call(kernel, out_shape=jax.ShapeDtypeStruct((TOK, WIDTH), BF16)...]
where the time goes in v5:
time: 65.4 us; the launch traced here: 65.2 us
  Pallas kernels  62.2 us (95%)
  local copies, waits for them, and re-layouts  3.05 us (5%)
    pallas_call x1, Pallas kernels, local(): pl.pallas_call(kernel, out_shape=jax.ShapeDtypeStruct((TOK, WIDTH), BF16)...  62.2 us
    unnamed x1, local copies, waits for them, and re-layouts  3.05 us

profile of v5, /device:TPU:1, one launch (start us, length us, event | category | flops | bytes accessed | tf_op | source)
XLA Modules:
  0.0 65.2 jit_solution(622554197042319773)
XLA Ops:
  0.0 62.2 %attention.1 = bf16[2048,512]{1,0:T(8,128)(2,1)} custom-call(bf16[512,512]{1,0:T(8,128)(2,1)} %gq_ref.1, bf16[512,512]{1,0:T(8,128)(2,1)} %gk_ref.1, s32[2,512]{1,0:T(2,128)} %span_ref.1, s32[2,2048]{1,0:T(2,128)} %doc_ref.1, bf16[2048,512]{1,0:T(8,128)(2,1)} %q_hbm.1, bf16[2048,512]{1,0:T(8,128)(2,1)} %k_hbm.1, bf16[2048,512]{1,0:T(8,128)(2,1)} %v_hbm.1, ...), custom_call_target="tpu_custom_call" | custom-call | tf_op jit(solution)/shard_map/attention/pallas_call | solution.py:461
  62.2 3.0 %copy.10 = bf16[2048,512]{1,0:T(8,128)(2,1)} copy(bf16[2048,512]{1,0:T(8,128)(2,1)} %attention.1) | data formatting | bytes 4194304

commit v6 on v5

--- a/solution.py
+++ b/solution.py
@@ -26,7 +26,7 @@
 PAIR = HERE // 2
 PIECES = 4
 PIECE = RADIUS // PIECES
-HALO_PLAN = (2, 0, 4, 1, 1)
+HALO_PLAN = (2, 1, 3, 1, 1)
 PARTS = PAIR + 1
 SIDE = WIDTH // 2
 MESH = pl.DeviceIdType.MESH

time: 65.4 us -> 63.4 us (0.969)
  Pallas kernels: 62.2 us -> 60.1 us
    pallas_call x1, Pallas kernels: 62.2 us -> 60.1 us  [local(): pl.pallas_call(kernel, out_shape=jax.ShapeDtypeStruct((TOK, WIDTH), BF16)...]
where the time goes in v6:
time: 63.4 us; the launch traced here: 63.2 us
  Pallas kernels  60.1 us (95%)
  local copies, waits for them, and re-layouts  3.05 us (5%)
    pallas_call x1, Pallas kernels, local(): pl.pallas_call(kernel, out_shape=jax.ShapeDtypeStruct((TOK, WIDTH), BF16)...  60.1 us
    unnamed x1, local copies, waits for them, and re-layouts  3.05 us

profile of v6, /device:TPU:1, one launch (start us, length us, event | category | flops | bytes accessed | tf_op | source)
XLA Modules:
  0.0 63.2 jit_solution(3019225754485577730)
XLA Ops:
  0.0 60.1 %attention.1 = bf16[2048,512]{1,0:T(8,128)(2,1)} custom-call(bf16[512,512]{1,0:T(8,128)(2,1)} %gq_ref.1, bf16[512,512]{1,0:T(8,128)(2,1)} %gk_ref.1, s32[2,512]{1,0:T(2,128)} %span_ref.1, s32[2,2048]{1,0:T(2,128)} %doc_ref.1, bf16[2048,512]{1,0:T(8,128)(2,1)} %q_hbm.1, bf16[2048,512]{1,0:T(8,128)(2,1)} %k_hbm.1, bf16[2048,512]{1,0:T(8,128)(2,1)} %v_hbm.1, ...), custom_call_target="tpu_custom_call" | custom-call | tf_op jit(solution)/shard_map/attention/pallas_call | solution.py:461
  60.1 3.0 %copy.10 = bf16[2048,512]{1,0:T(8,128)(2,1)} copy(bf16[2048,512]{1,0:T(8,128)(2,1)} %attention.1) | data formatting | bytes 4194304

commit v7 on v6

--- a/solution.py
+++ b/solution.py
@@ -401,15 +401,6 @@
     def _(i):
         own_keys(i * (TILES - 1), RADIUS + i * (TOK - far), far, 2 + i)
 
-    for c in range(2 * PIECES):
-        for copy in halo_pair(c):
-            copy.wait_recv()
-
-    @pl.loop(0, 2)
-    def _(i):
-        halo_keys(1 + i * (TILES - 3), TILE + i * (TOK + TILE), TILE, i)
-        halo_keys(i * (TILES - 1), i * (TOK + RADIUS), RADIUS, 2 + i)
-
     for half in range(2):
         for d in range(1, NX):
             second_copy(half, d).wait_recv()
@@ -433,6 +424,15 @@
     @pl.loop(first_in, last_in)
     def _(t):
         finish(t, None)
+
+    for c in range(2 * PIECES):
+        for copy in halo_pair(c):
+            copy.wait_recv()
+
+    @pl.loop(0, 2)
+    def _(i):
+        halo_keys(1 + i * (TILES - 3), TILE + i * (TOK + TILE), TILE, i)
+        halo_keys(i * (TILES - 1), i * (TOK + RADIUS), RADIUS, 2 + i)
 
     @pl.loop(0, 2)
     def _(i):

time: 63.4 us -> 61.9 us (0.976)
  Pallas kernels: 60.1 us -> 58.3 us
    pallas_call x1, Pallas kernels: 60.1 us -> 58.3 us  [local(): pl.pallas_call(kernel, out_shape=jax.ShapeDtypeStruct((TOK, WIDTH), BF16)...]
where the time goes in v7:
time: 61.9 us; the launch traced here: 61.4 us
  Pallas kernels  58.3 us (94%)
  local copies, waits for them, and re-layouts  3.05 us (5%)
    pallas_call x1, Pallas kernels, local(): pl.pallas_call(kernel, out_shape=jax.ShapeDtypeStruct((TOK, WIDTH), BF16)...  58.3 us
    unnamed x1, local copies, waits for them, and re-layouts  3.05 us

profile of v7, /device:TPU:1, one launch (start us, length us, event | category | flops | bytes accessed | tf_op | source)
XLA Modules:
  0.0 61.4 jit_solution(2443589817398149915)
XLA Ops:
  0.0 58.3 %attention.1 = bf16[2048,512]{1,0:T(8,128)(2,1)} custom-call(bf16[512,512]{1,0:T(8,128)(2,1)} %gq_ref.1, bf16[512,512]{1,0:T(8,128)(2,1)} %gk_ref.1, s32[2,512]{1,0:T(2,128)} %span_ref.1, s32[2,2048]{1,0:T(2,128)} %doc_ref.1, bf16[2048,512]{1,0:T(8,128)(2,1)} %q_hbm.1, bf16[2048,512]{1,0:T(8,128)(2,1)} %k_hbm.1, bf16[2048,512]{1,0:T(8,128)(2,1)} %v_hbm.1, ...), custom_call_target="tpu_custom_call" | custom-call | tf_op jit(solution)/shard_map/attention/pallas_call | solution.py:461
  58.3 3.0 %copy.10 = bf16[2048,512]{1,0:T(8,128)(2,1)} copy(bf16[2048,512]{1,0:T(8,128)(2,1)} %attention.1) | data formatting | bytes 4194304
